TPU v7x, 128 devices: a whole 4x4x4 slice. The times are simulated.
128 devices in a mesh: row: 4 (over y), col: 32 (over x, z, core).
Axes of the slice: x: 4, y: 4, z: 4, core: 2. Of those that a mesh axis runs over, the one named last changes fastest.
Arguments:
- left_site: bfloat16 [4096, 2048], P('row', 'col')
- right_site: bfloat16 [2048, 4096], P('row', 'col'), may hold values from -0.125 to 0.125
- gate: float32 [4, 4], replicated, may hold values from -0.6 to 2.1
- omega: bfloat16 [4096, 2304], P(None, 'row'), may hold values from -0.09375 to 0.09375
Outputs:
- basis: float32 [4096, 2304], P(('row', 'col'))
- projected: float32 [2304, 4096], P('row', 'col')
All inputs are finite; a program needn't handle non-finite values.
Results may differ from a plain program's by a relative error of at most 0.0085.
Values may be sent and summed in bfloat16 or wider, within the bound.
A program may use at most 192 MiB of HBM per device.

v0:
```python
import math

import jax
import jax.numpy as jnp
from jax import lax
from jax.sharding import PartitionSpec as P


def apply_gate(bare, gate):
    row_count, col_count = bare.shape
    paired = bare.reshape(row_count // 2, 2, col_count)
    lanes = jnp.arange(col_count)
    same_pair = lanes[:, None] // 2 == lanes[None, :] // 2
    source_bit = lanes[:, None] % 2
    target_bit = lanes[None, :] % 2
    gate_four = gate.reshape(2, 2, 2, 2)
    outputs = []
    for first_state in range(2):
        running = jnp.zeros((row_count // 2, col_count), jnp.float32)
        for source_state in range(2):
            coupling = gate_four[first_state, :, source_state, :]
            mixer = jnp.zeros((col_count, col_count), jnp.float32)
            for second_state in range(2):
                for other_state in range(2):
                    hit = same_pair & (target_bit == second_state) & (source_bit == other_state)
                    mixer = mixer + jnp.where(hit, coupling[second_state, other_state], 0.0)
            running = running + jnp.dot(
                paired[:, source_state, :], mixer, precision=lax.Precision.HIGHEST
            )
        outputs.append(running)
    return jnp.stack(outputs, axis=1).reshape(row_count, col_count)


def split_product(factor_rows, theta_rows):
    head = factor_rows.astype(jnp.bfloat16)
    rest = (factor_rows - head.astype(jnp.float32)).astype(jnp.bfloat16)
    dims = (((0,), (0,)), ((), ()))
    first = lax.dot_general(head, theta_rows, dims, preferred_element_type=jnp.float32)
    second = lax.dot_general(rest, theta_rows, dims, preferred_element_type=jnp.float32)
    return first + second


def gram_cross(upper_part, lower_part):
    return jnp.dot(upper_part.T, lower_part, precision=lax.Precision.HIGHEST)


def gram_blocks(sketch):
    third = sketch.shape[1] // 3
    part_one = sketch[:, :third]
    part_two = sketch[:, third : 2 * third]
    part_three = sketch[:, 2 * third :]
    return (
        gram_cross(part_one, part_one),
        gram_cross(part_one, part_two),
        gram_cross(part_one, part_three),
        gram_cross(part_two, part_two),
        gram_cross(part_two, part_three),
        gram_cross(part_three, part_three),
    )


def exact_dot(first, second):
    return jnp.dot(first, second, precision=lax.Precision.HIGHEST)


def right_solve(lower_block, values):
    return jax.scipy.linalg.solve_triangular(lower_block, values.T, lower=True).T


def factor_of(blocks, total_rows):
    scaled = [block / total_rows for block in blocks]
    diag_one = jnp.linalg.cholesky(scaled[0])
    below_one = right_solve(diag_one, scaled[1].T)
    bottom_one = right_solve(diag_one, scaled[2].T)
    diag_two = jnp.linalg.cholesky(scaled[3] - exact_dot(below_one, below_one.T))
    bottom_two = right_solve(diag_two, scaled[4].T - exact_dot(bottom_one, below_one.T))
    rest_three = (
        scaled[5] - exact_dot(bottom_one, bottom_one.T) - exact_dot(bottom_two, bottom_two.T)
    )
    diag_three = jnp.linalg.cholesky(rest_three)
    return (diag_one, below_one, bottom_one, diag_two, bottom_two, diag_three)


def basis_of(factor, sketch):
    third = sketch.shape[1] // 3
    first_cols = right_solve(factor[0], sketch[:, :third])
    second_cols = right_solve(
        factor[3], sketch[:, third : 2 * third] - exact_dot(first_cols, factor[1].T)
    )
    third_cols = (
        sketch[:, 2 * third :]
        - exact_dot(first_cols, factor[2].T)
        - exact_dot(second_cols, factor[4].T)
    )
    third_cols = right_solve(factor[5], third_cols)
    return jnp.concatenate([first_cols, second_cols, third_cols], axis=1)


def on_device(left_site, right_site, gate, omega):
    rows_here = left_site.shape[0]
    total_rows = rows_here * lax.axis_size("row")
    right_cols = lax.all_gather(right_site, "row", axis=0, tiled=True)
    cols_here = right_cols.shape[1]
    bare = jnp.dot(
        lax.all_gather(left_site, "col", axis=1, tiled=True),
        right_cols,
        preferred_element_type=jnp.float32,
    )
    theta = apply_gate(bare, gate).astype(jnp.bfloat16)
    col_start = lax.axis_index("col") * cols_here
    omega_mine = lax.dynamic_slice_in_dim(omega, col_start, cols_here, 0)
    omega_rows = lax.all_gather(omega_mine, "row", axis=1, tiled=True)
    theta_rows = theta
    sketch = lax.psum_scatter(
        jnp.dot(theta_rows, omega_rows, preferred_element_type=jnp.float32),
        "col",
        scatter_dimension=0,
        tiled=True,
    )
    blocks = lax.psum(gram_blocks(sketch), ("row", "col"))
    factor = factor_of(blocks, total_rows)
    basis = basis_of(factor, sketch)
    theta_rows = theta
    folded = split_product(lax.all_gather(basis, "col", axis=0, tiled=True), theta_rows)
    projected = lax.psum_scatter(folded, "row", scatter_dimension=0, tiled=True) / math.sqrt(
        total_rows
    )
    return (basis, projected)


def solution(mesh):
    in_specs = (P("row", "col"), P("row", "col"), P(), P(None, "row"))
    out_specs = (P(("row", "col"), None), P("row", "col"))
    return jax.shard_map(
        on_device, mesh=mesh, in_specs=in_specs, out_specs=out_specs, check_vma=False
    )
```

profile of v0, /device:TPU:0, one launch (start us, length us, event | category | flops | bytes accessed | tf_op | source)
XLA Modules:
  0.0 1310.0 jit_solution(17415036318952621000)
XLA Ops:
  12.3 13.6 %all_gather.13 = bf16[2048,128]{1,0:T(8,128)(2,1)S(1)} all-gather(bf16[512,128]{1,0:T(8,128)(2,1)} %param.10), channel_id=1, replica_groups=mesh['row'=4,'col'=32] {'row'}, dimensions={0}, use_global_device_ids=true | all-gather | bytes 655360 | tf_op jit(solution)/shard_map/all_gather | solution.py:102
  25.9 13.4 %all_gather.14 = bf16[128,2304]{0,1:T(8,128)(2,1)S(1)} all-gather(bf16[128,576]{0,1:T(8,128)(2,1)S(1)} %constant_dynamic-slice_fusion.3), channel_id=1, replica_groups=mesh['row'=4,'col'=32] {'row'}, dimensions={1}, use_global_device_ids=true | all-gather | bytes 737280 | tf_op jit(solution)/shard_map/all_gather | solution.py:112
  39.4 19.6 %all-gather.3.cloned.1.call-done = bf16[1024,2048]{0,1:T(8,128)(2,1)} async-done(((bf16[1024,64]{0,1:T(8,128)(2,1)}), bf16[1024,2048]{0,1:T(8,128)(2,1)}) %all-gather.3.cloned.1.call-update) | async-done | bytes 4194320 | tf_op jit(solution)/shard_map/all_gather | solution.py:105
  80.5 94.6 %reduce-scatter.3.cloned.1.call-done = f32[32,2304]{1,0:T(8,128)} async-done(((f32[1024,2304]{1,0:T(8,128)}), f32[32,2304]{1,0:T(8,128)}) %reduce-scatter.3.cloned.1.call-update) | async-done | bytes 294928 | tf_op jit(solution)/shard_map/reduce_scatter | solution.py:114
  197.7 172.9 %all-reduce.4.cloned.1.call-done = (f32[768,768]{0,1:T(8,128)}, f32[768,768]{0,1:T(8,128)}, f32[768,768]{0,1:T(8,128)}, f32[768,768]{0,1:T(8,128)}, f32[768,768]{0,1:T(8,128)}, /*index=5*/f32[768,768]{0,1:T(8,128)}) async-done(((f32[768,768]{0,1:T(8,128)}, f32[768,768]{0,1:T(8,128)}, f32[768,768]{0,1:T(8,128)}, f32[768,768]{0,1:T(8,128)}, f32[768,768]{0,1:T(8,128)}, /*index=5*/f32[768,768]{0,1:T(8,128)}), ...) | async-done | bytes 14155792 | tf_op jit(solution)/shard_map/psum | solution.py:120
  380.6 11.7 cholesky.591
  405.1 11.7 cholesky.610
  430.2 11.7 cholesky.631
  454.3 12.1 cholesky.650
  478.7 11.7 cholesky.669
  502.5 11.8 cholesky.686
  520.5 17.5 %while.12 = (s32[]{:T(128)}, f32[768,768]{1,0:T(8,128)}, s32[6,2]{0,1:T(2,128)S(1)}, f32[6,128,128]{2,1,0:T(8,128)S(1)}, s32[]{:T(128)}) while((s32[]{:T(128)}, f32[768,768]{1,0:T(8,128)}, s32[6,2]{0,1:T(2,128)S(1)}, f32[6,128,128]{2,1,0:T(8,128)S(1)}, s32[]{:T(128)}) %tuple.169), condition=%wide.while_cond, body=%wide.while_body.sunk | while | flops 2 | bytes 131181 | solution.py:67
  537.9 59.0 %custom-call.57 = f32[6,128,128]{1,2,0:T(8,128)S(1)} custom-call(f32[6,128,128]{2,1,0:T(8,128)S(1)} %get-tuple-element.45), custom_call_target="InvertDiagBlocksLowerTriangular" | custom-call | tf_op jit(solution)/shard_map/jit(_solve_triangular)/triangular_solve | solution.py:67
  657.7 11.7 cholesky.701
  685.2 11.7 cholesky.720
  713.4 11.7 cholesky.741
  740.8 13.6 %cholesky.760 = f32[128,128]{1,0:T(8,128)} custom-call(f32[128,128]{1,0:T(8,128)} %cholesky.954), custom_call_target="Cholesky" | custom-call | tf_op jit(solution)/shard_map/jit(cholesky)/cholesky | solution.py:75
  771.3 12.3 cholesky.779
  799.5 11.9 cholesky.796
  820.4 21.0 %while.13 = (s32[]{:T(128)}, f32[768,768]{1,0:T(8,128)}, s32[6,2]{0,1:T(2,128)S(1)}, f32[6,128,128]{2,1,0:T(8,128)}, s32[]{:T(128)}) while((s32[]{:T(128)}, f32[768,768]{1,0:T(8,128)}, s32[6,2]{0,1:T(2,128)S(1)}, f32[6,128,128]{2,1,0:T(8,128)}, s32[]{:T(128)}) %tuple.189), condition=%wide.while_cond.clone, body=%wide.while_body.clone.sunk | while | flops 2 | bytes 132705 | solution.py:67
  841.5 60.4 %custom-call.64 = f32[6,128,128]{1,2,0:T(8,128)} custom-call(f32[6,128,128]{2,1,0:T(8,128)} %get-tuple-element.47), custom_call_target="InvertDiagBlocksLowerTriangular" | custom-call | tf_op jit(solution)/shard_map/jit(_solve_triangular)/triangular_solve | solution.py:67
  939.1 11.7 cholesky.811
  966.6 11.7 cholesky.830
  995.0 11.7 cholesky.851
  1022.3 13.6 %cholesky.870 = f32[128,128]{1,0:T(8,128)} custom-call(f32[128,128]{1,0:T(8,128)} %cholesky.977), custom_call_target="Cholesky" | custom-call | tf_op jit(solution)/shard_map/jit(cholesky)/cholesky | solution.py:80
  1038.1 11.3 custom-call.70
  1052.9 12.3 cholesky.889
  1081.1 11.9 cholesky.906
  1102.3 21.2 %while.14 = (s32[]{:T(128)}, f32[768,768]{1,0:T(8,128)}, s32[6,2]{0,1:T(2,128)S(1)}, f32[6,128,128]{2,1,0:T(8,128)}, s32[]{:T(128)}) while((s32[]{:T(128)}, f32[768,768]{1,0:T(8,128)}, s32[6,2]{0,1:T(2,128)S(1)}, f32[6,128,128]{2,1,0:T(8,128)}, s32[]{:T(128)}) %tuple.190), condition=%wide.while_cond.clone.1, body=%wide.while_body.clone.1.sunk | while | flops 2 | bytes 132705 | solution.py:67
  1123.5 60.4 %custom-call.72 = f32[6,128,128]{1,2,0:T(8,128)} custom-call(f32[6,128,128]{2,1,0:T(8,128)} %get-tuple-element.50), custom_call_target="InvertDiagBlocksLowerTriangular" | custom-call | tf_op jit(solution)/shard_map/jit(_solve_triangular)/triangular_solve | solution.py:67
  1212.7 53.5 %all-gather.5.cloned.1.call-done = f32[1024,2304]{1,0:T(8,128)} async-done(((f32[32,2304]{1,0:T(8,128)}), f32[1024,2304]{1,0:T(8,128)}) %all-gather.5.cloned.1.call-update) | async-done | bytes 9437200 | tf_op jit(solution)/shard_map/all_gather | solution.py:124
  1277.7 23.9 %reduce-scatter.5.cloned.1.call-done = f32[576,128]{1,0:T(8,128)} async-done(((f32[2304,128]{1,0:T(8,128)}), f32[576,128]{1,0:T(8,128)}) %reduce-scatter.5.cloned.1.call-update) | async-done | bytes 294928 | tf_op jit(solution)/shard_map/reduce_scatter | solution.py:125
  (329 shorter events, 484.2 us)
Async XLA Ops:
  7.2 51.8 %all-gather.3.cloned.1.call-start = ((), (), s32[]{:S(2)}) async-start(), calls=%async_computation.2 | async-start | bytes 4325376 | tf_op jit(solution)/shard_map/all_gather | solution.py:105
  7.9 167.2 %reduce-scatter.3.cloned.1.call-start = ((), (), s32[]{:S(2)}) async-start(), calls=%async_computation.3 | async-start | bytes 9732096 | tf_op jit(solution)/shard_map/reduce_scatter | solution.py:114
  80.0 290.6 %all-reduce.4.cloned.1.call-start = ((), (), s32[]{:S(2)}) async-start(), calls=%async_computation.6 | async-start | bytes 28311552 | tf_op jit(solution)/shard_map/psum | solution.py:120
  175.1 4.4 copy-start.11
  197.0 1069.2 %all-gather.5.cloned.1.call-start = ((), (), s32[]{:S(2)}) async-start(), calls=%async_computation.4 | async-start | bytes 9732096 | tf_op jit(solution)/shard_map/all_gather | solution.py:124
  373.8 3.4 copy-start.6
  379.2 1.4 copy-start.8
  596.9 2.5 copy-start.5
  608.0 4.3 copy-start.12
  626.2 8.0 copy-start.15
  634.2 7.9 copy-start.1
  634.3 7.9 copy-start.14
  656.3 1.5 copy-start.9
  684.4 0.7 copy-start.18
  712.7 0.7 copy-start.20
  901.9 3.6 copy-start.16
  901.9 4.1 copy-start.7
  916.0 7.5 copy-start.4
  916.0 7.5 copy-start.13
  922.1 1.4 copy-start.2
  937.6 1.4 copy-start.10
  965.9 0.7 copy-start.19
  994.2 0.7 copy-start.21
  1098.2 85.7 %copy-start.22 = (f32[768,32]{0,1:T(8,128)S(1)}, f32[768,32]{0,1:T(8,128)}, u32[]{:S(2)}) copy-start(f32[768,32]{0,1:T(8,128)} %slice_bitcast_fusion) | copy-start | bytes 294916
  1184.0 10.3 copy-start.17
  1194.5 8.7 copy-start.3
  1201.7 2.9 copy-start.23
  1212.7 88.9 %reduce-scatter.5.cloned.1.call-start = ((), (), s32[]{:S(2)}) async-start(), calls=%async_computation.5 | async-start | bytes 1474560 | tf_op jit(solution)/shard_map/reduce_scatter | solution.py:125
  1266.2 9.0 copy-start
Sparse Core Ops, SparseCore 0:
  10.2 48.6 all-gather.2
  80.1 94.9 reduce-scatter.2
  197.1 173.4 all-reduce.3
  1212.8 53.3 all-gather.4
  1277.9 23.7 reduce-scatter.4
where the time goes:
time: 1320 us; the launch traced here: 1310 us
  other arithmetic  594 us (45%)
  waiting for transfers between devices  365 us (28%)
  matrix products  205 us (16%)
  local copies, waits for them, and re-layouts  91.4 us (7%)
  blocking collectives  27.1 us (2%)
  between operations  26.6 us (2%)
    another operation x7, other arithmetic, right_solve(): jax.scipy.linalg.solve_triangular(lower_block, values.T, lower=True)  188 us
    psum x1, waiting for transfers between devices, on_device(): blocks = lax.psum(gram_blocks(sketch), ('row', 'col'))  173 us
    another operation x23, other arithmetic, factor_of(): diag_three = jnp.linalg.cholesky(rest_three)  133 us
    another operation x23, other arithmetic, factor_of(): jnp.linalg.cholesky(scaled[3] - exact_dot(below_one, below_one.T))  133 us
    another operation x23, other arithmetic, factor_of(): diag_one = jnp.linalg.cholesky(scaled[0])  124 us
    reduce_scatter x1, waiting for transfers between devices, on_device(): lax.psum_scatter(jnp.dot(theta_rows, omega_rows, preferred_element_type=j...  94.6 us
    another operation x66, matrix products, right_solve(): jax.scipy.linalg.solve_triangular(lower_block, values.T, lower=True)  69.3 us
    another operation x58, local copies, waits for them, and re-layouts, right_solve(): jax.scipy.linalg.solve_triangular(lower_block, values.T, lower=True)  61.2 us
  transfers between devices with their start and end apart: 5, of which 5 were waited for; matrix products, arithmetic and copies ran while one was open for 0% of the time, Pallas kernels for 0%

commit v1 on v0

v1 whole, which is shorter than its diff:
```python
import functools

import jax
import jax.numpy as jnp
import numpy as np
from jax import lax
from jax.experimental import pallas as pl
from jax.experimental.pallas import tpu as pltpu
from jax.sharding import Mesh
from jax.sharding import PartitionSpec as P

HI = lax.Precision.HIGHEST
F32, BF16 = jnp.float32, jnp.bfloat16
TILE = 256
HALF = 128
VMEM_LIMIT = 60 << 20
WHOLE = pl.BlockSpec(memory_space=pltpu.VMEM)


def split(x):
    head = x.astype(BF16)
    return head, (x - head.astype(F32)).astype(BF16)


def tdot(a, b, precision=None):
    return lax.dot_general(
        a, b, (((0,), (0,)), ((), ())), preferred_element_type=F32, precision=precision
    )


def front_kernel(gate_ref, left_ref, right_ref, omega_ref, theta_ref, sketch_ref, bond_ref):
    groups, lanes_x, part, rows = left_ref.shape
    for xs in range(lanes_x):
        for zc in range(groups):
            at = (xs * groups + zc) * part
            bond_ref[at : at + part, :] = left_ref[zc, xs]
    width = right_ref.shape[2]
    left = bond_ref[...]
    row_odd = lax.broadcasted_iota(jnp.int32, (rows, width), 0) % 2 == 1
    col_odd = lax.broadcasted_iota(jnp.int32, (rows, width), 1) % 2 == 1

    def coupling(row_flip, col_flip):
        def entry(s1, s2):
            a, b = s1 ^ row_flip, s2 ^ col_flip
            return gate_ref[2 * s1 + s2, 2 * a + b]

        even = jnp.where(col_odd, entry(0, 1), entry(0, 0))
        odd = jnp.where(col_odd, entry(1, 1), entry(1, 0))
        return jnp.where(row_odd, odd, even)

    for xs in range(right_ref.shape[0]):
        bare = tdot(left, right_ref[xs])
        row_partner = jnp.where(row_odd, pltpu.roll(bare, 1, 0), pltpu.roll(bare, rows - 1, 0))

        def col_partner(v):
            return jnp.where(col_odd, pltpu.roll(v, 1, 1), pltpu.roll(v, width - 1, 1))

        mixed = (coupling(0, 0) * bare + coupling(0, 1) * col_partner(bare)) + (
            coupling(1, 0) * row_partner + coupling(1, 1) * col_partner(row_partner)
        )
        theta_ref[:, xs * width : (xs + 1) * width] = mixed.astype(BF16)
    theta = theta_ref[...]
    step = omega_ref.shape[2]
    for y in range(omega_ref.shape[0]):
        sketch_ref[:, y * step : (y + 1) * step] = jnp.dot(
            theta, omega_ref[y], preferred_element_type=F32
        )


def front(gate, left, right, omega):
    rows = left.shape[3]
    bond = right.shape[1]
    cols = right.shape[0] * right.shape[2]
    k = omega.shape[0] * omega.shape[2]
    return pl.pallas_call(
        front_kernel,
        out_shape=(jax.ShapeDtypeStruct((rows, cols), BF16), jax.ShapeDtypeStruct((rows, k), F32)),
        in_specs=[pl.BlockSpec(memory_space=pltpu.SMEM), WHOLE, WHOLE, WHOLE],
        out_specs=(WHOLE, WHOLE),
        scratch_shapes=[pltpu.VMEM((bond, rows), BF16)],
        compiler_params=pltpu.CompilerParams(vmem_limit_bytes=VMEM_LIMIT),
        name="front",
    )(gate, left, right, omega)


def gram_kernel(scale, per, group_ref, i_ref, j_ref, s_ref, out_ref):
    chunks, piece = out_ref.shape[0], out_ref.shape[2]

    def tile(t, carry):
        at = group_ref[0] * per + t
        i = pl.multiple_of(i_ref[at] * TILE, TILE)
        j = pl.multiple_of(j_ref[at] * TILE, TILE)
        value = tdot(s_ref[:, pl.ds(i, TILE)], s_ref[:, pl.ds(j, TILE)], HI) * scale
        out_ref[:, pl.ds(t, 1)] = value.reshape(chunks, 1, piece, TILE)
        return carry

    lax.fori_loop(0, per, tile, 0)


def gram(sketch, group, pairs, per, chunks, scale):
    smem = pl.BlockSpec(memory_space=pltpu.SMEM)
    return pl.pallas_call(
        functools.partial(gram_kernel, scale, per),
        out_shape=jax.ShapeDtypeStruct((chunks, per, TILE // chunks, TILE), F32),
        in_specs=[smem, smem, smem, WHOLE],
        out_specs=WHOLE,
        compiler_params=pltpu.CompilerParams(vmem_limit_bytes=VMEM_LIMIT),
        name="gram",
    )(group, pairs[0], pairs[1], sketch)


def cross_kernel(scale, s_ref, theta_ref, out_ref):
    parts, _, width = out_ref.shape
    for at in range(0, s_ref.shape[1], TILE):
        head, rest = split(s_ref[:, at : at + TILE])
        value = (tdot(head, theta_ref[...]) + tdot(rest, theta_ref[...])) * scale
        for x in range(parts):
            out_ref[x, at : at + TILE, :] = value[:, x * width : (x + 1) * width]


def cross(sketch, theta, parts, scale):
    width = theta.shape[1] // parts
    return pl.pallas_call(
        functools.partial(cross_kernel, scale),
        out_shape=jax.ShapeDtypeStruct((parts, sketch.shape[1], width), F32),
        in_specs=[WHOLE, WHOLE],
        out_specs=WHOLE,
        compiler_params=pltpu.CompilerParams(vmem_limit_bytes=VMEM_LIMIT),
        name="cross",
    )(sketch, theta)


def leaf(rows):
    lane = lax.broadcasted_iota(jnp.int32, (8, HALF), 1)
    sub = lax.broadcasted_iota(jnp.int32, (8, HALF), 0)
    rows = list(rows)
    count = len(rows)
    done = []
    for j in range(count):
        base = 8 * j
        here = (lane >= base) & (lane < base + 8)
        part = rows[j]
        cols = [jnp.broadcast_to(part[:, base + k : base + k + 1], (8, HALF)) for k in range(8)]
        part = jnp.where(here, jnp.where(lane - base == sub, 1.0, 0.0), part)
        tri = jnp.zeros((8, HALF), F32)
        for k in range(8):
            at = sub == k
            pivot = jnp.broadcast_to(cols[k][k : k + 1, :], (8, HALF))
            inv = 1.0 / pivot
            row = jnp.broadcast_to(part[k : k + 1, :], (8, HALF))
            tri = jnp.where(at, row * lax.rsqrt(pivot), tri)
            factor = cols[k] * inv
            part = jnp.where(at, row * inv, part - factor * row)
            for m in range(k + 1, 8):
                mrow = jnp.broadcast_to(cols[m][k : k + 1, :], (8, HALF))
                cols[m] = jnp.where(at, mrow * inv, cols[m] - factor * mrow)
        done.append(jnp.where(lane < base + 8, tri, 0.0))
        if j + 1 < count:
            prow = [jnp.broadcast_to(part[k : k + 1, :], (8, HALF)) for k in range(8)]
            for i in range(j + 1, count):
                mine = rows[i]
                terms = [
                    jnp.broadcast_to(mine[:, base + k : base + k + 1], (8, HALF)) * prow[k]
                    for k in range(8)
                ]
                while len(terms) > 1:
                    terms = [terms[q] + terms[q + 1] for q in range(0, len(terms), 2)]
                rows[i] = jnp.where(here, 0.0, mine) - terms[0]
    return done


def factor_kernel(
    pairs, per, g_ref, uh_ref, ul_ref, inv_ref, grid_ref, a_ref, l1_ref, l2_ref, sem
):
    blocks, piece, n = grid_ref.shape
    t_ref = grid_ref.reshape(n, n)
    nt = n // TILE
    chunks = TILE // piece
    groups = g_ref.shape[0] // chunks
    source = g_ref.reshape(chunks, groups, per, piece, TILE)

    def fetch(at):
        i, j = pairs[at]
        return pltpu.make_async_copy(
            source.at[:, at // per, at % per],
            grid_ref.at[pl.ds(i * chunks, chunks), :, pl.ds(j * TILE, TILE)],
            sem.at[min(i, 1)],
        )

    for at in range(len(pairs)):
        fetch(at).start()
    for at in range(len(pairs)):
        if pairs[at][0] == 0:
            fetch(at).wait()

    def factor(l_ref):
        out = leaf([a_ref[8 * i : 8 * i + 8, :] for i in range(HALF // 8)])
        for i, rows in enumerate(out):
            l_ref[8 * i : 8 * i + 8, :] = rows

    def panel(p, carry):
        base = pl.multiple_of(p * TILE, TILE)
        mid = pl.multiple_of(p * TILE + HALF, HALF)
        a_ref[...] = t_ref[pl.ds(base, HALF), pl.ds(base, HALF)]
        factor(l1_ref)
        l1 = l1_ref[...]
        uab = jnp.dot(l1, t_ref[pl.ds(base, HALF), pl.ds(mid, HALF)], precision=HI)
        a_ref[...] = t_ref[pl.ds(mid, HALF), pl.ds(mid, HALF)] - tdot(uab, uab, HI)
        factor(l2_ref)
        l2 = l2_ref[...]
        l21 = -jnp.dot(l2, tdot(uab, l1, HI), precision=HI)
        inv_ref[p, 0:HALF, 0:HALF] = l1
        inv_ref[p, 0:HALF, HALF:] = jnp.zeros((HALF, HALF), F32)
        inv_ref[p, HALF:, 0:HALF] = l21
        inv_ref[p, HALF:, HALF:] = l2

        @pl.when(p == 0)
        def _():
            for at in range(len(pairs)):
                if pairs[at][0] != 0:
                    fetch(at).wait()

        def row_tile(c, carry):
            at = pl.multiple_of(c * TILE, TILE)
            u = jnp.dot(inv_ref[p], t_ref[pl.ds(base, TILE), pl.ds(at, TILE)], precision=HI)
            head, rest = split(u)
            uh_ref[pl.ds(base, TILE), pl.ds(at, TILE)] = head
            ul_ref[pl.ds(base, TILE), pl.ds(at, TILE)] = rest
            return carry

        lax.fori_loop(p + 1, nt, row_tile, 0)

        def trail_row(r, carry):
            rat = pl.multiple_of(r * TILE, TILE)
            head = uh_ref[pl.ds(base, TILE), pl.ds(rat, TILE)].T
            rest = ul_ref[pl.ds(base, TILE), pl.ds(rat, TILE)].T

            def trail(c, carry):
                cat = pl.multiple_of(c * TILE, TILE)
                ch = uh_ref[pl.ds(base, TILE), pl.ds(cat, TILE)]
                cl = ul_ref[pl.ds(base, TILE), pl.ds(cat, TILE)]
                update = jnp.dot(head, ch, preferred_element_type=F32) + (
                    jnp.dot(head, cl, preferred_element_type=F32)
                    + jnp.dot(rest, ch, preferred_element_type=F32)
                )
                t_ref[pl.ds(rat, TILE), pl.ds(cat, TILE)] -= update
                return carry

            lax.fori_loop(r, nt, trail, 0)
            return carry

        lax.fori_loop(p + 1, nt, trail_row, 0)
        return carry

    lax.fori_loop(0, nt, panel, 0)


def factorize(tiles, n, pairs, per):
    piece = tiles.shape[2]
    return pl.pallas_call(
        functools.partial(factor_kernel, pairs, per),
        out_shape=(
            jax.ShapeDtypeStruct((n, n), BF16),
            jax.ShapeDtypeStruct((n, n), BF16),
            jax.ShapeDtypeStruct((n // TILE, TILE, TILE), F32),
        ),
        in_specs=[pl.BlockSpec(memory_space=pl.ANY)],
        out_specs=(WHOLE,) * 3,
        scratch_shapes=[
            pltpu.VMEM((n // piece, piece, n), F32),
            pltpu.VMEM((HALF, HALF), F32),
            pltpu.VMEM((HALF, HALF), F32),
            pltpu.VMEM((HALF, HALF), F32),
            pltpu.SemaphoreType.DMA((2,)),
        ],
        compiler_params=pltpu.CompilerParams(vmem_limit_bytes=VMEM_LIMIT),
        cost_estimate=pl.CostEstimate(
            flops=2 * n**3, bytes_accessed=n * n * 8, transcendentals=0
        ),
        name="factorize",
    )(tiles)


def solve_kernel(nt, uh_ref, ul_ref, inv_ref, s_ref, w_ref, basis_ref, proj_ref, y_ref):
    p = pl.program_id(0)
    mine, n = s_ref.shape

    @pl.when(p == 0)
    def _():
        padded = jnp.concatenate([s_ref[...], jnp.zeros((HALF - mine, n), F32)], axis=0)
        y_ref[:, :HALF] = padded.T
        y_ref[:, HALF:] = w_ref[...]

    base = pl.multiple_of(p * TILE, TILE)
    y = jnp.dot(inv_ref[0], y_ref[pl.ds(base, TILE), :], precision=HI)
    y_ref[pl.ds(base, TILE), :] = y
    proj_ref[pl.ds(base, TILE), :] = y[:, HALF:]
    head, rest = split(y)

    def tail(r, carry):
        at = pl.multiple_of(r * TILE, TILE)
        uh = uh_ref[:, pl.ds(at, TILE)]
        ul = ul_ref[:, pl.ds(at, TILE)]
        y_ref[pl.ds(at, TILE), :] -= tdot(uh, head) + (tdot(uh, rest) + tdot(ul, head))
        return carry

    lax.fori_loop(p + 1, nt, tail, 0)

    @pl.when(p == nt - 1)
    def _():
        basis_ref[...] = y_ref[:, :HALF].T[:mine]


def solve(uh, ul, inv, sketch, weights):
    mine, n = sketch.shape
    nt = n // TILE
    fixed = lambda p: (0, 0)
    return pl.pallas_call(
        functools.partial(solve_kernel, nt),
        grid=(nt,),
        out_shape=(jax.ShapeDtypeStruct((mine, n), F32), jax.ShapeDtypeStruct((n, HALF), F32)),
        in_specs=[
            pl.BlockSpec((TILE, n), lambda p: (p, 0)),
            pl.BlockSpec((TILE, n), lambda p: (p, 0)),
            pl.BlockSpec((1, TILE, TILE), lambda p: (p, 0, 0)),
            pl.BlockSpec((mine, n), fixed),
            pl.BlockSpec((n, HALF), fixed),
        ],
        out_specs=(pl.BlockSpec((mine, n), fixed), pl.BlockSpec((n, HALF), fixed)),
        scratch_shapes=[pltpu.VMEM((n, 2 * HALF), F32)],
        compiler_params=pltpu.CompilerParams(vmem_limit_bytes=VMEM_LIMIT),
        name="solve",
    )(uh, ul, inv, sketch, weights)


def tile_pairs(nt, groups):
    pairs = [(i, j) for i in range(nt) for j in range(i, nt)]
    per = -(-len(pairs) // groups)
    return pairs, per


def on_device(left_site, right_site, gate, omega):
    ny, nx, nz, nc = (lax.axis_size(a) for a in ("row", "x", "z", "core"))
    groups = nz * nc
    rows_y, part = left_site.shape
    rows = rows_y // nx
    total = rows_y * ny
    zc = lax.axis_index("z") * nc + lax.axis_index("core")

    left = left_site.T.reshape(part, nx, rows).transpose(1, 0, 2)
    left = lax.all_to_all(left, "x", 0, 0)
    left = lax.all_gather(left, ("z", "core"), axis=0)
    right = lax.all_gather(right_site, "row", axis=0, tiled=True)
    right = lax.all_gather(right, "x", axis=0)
    width = right_site.shape[1]
    omega_mine = lax.dynamic_slice_in_dim(
        omega.reshape(nx, groups, width, omega.shape[1]), zc, 1, 1
    ).reshape(nx * width, omega.shape[1])
    omega_all = lax.all_gather(omega_mine, "row", axis=0)

    theta, partial = front(gate, left, right, omega_all)
    sketch = lax.psum_scatter(partial, ("z", "core"), scatter_dimension=0, tiled=True)
    n = sketch.shape[1]
    sketch_rows = lax.all_gather(sketch, ("z", "core"), axis=0, tiled=True)

    pairs, per = tile_pairs(n // TILE, groups)
    padded = pairs + [(0, 0)] * (per * groups - len(pairs))
    table = jnp.asarray(np.array(padded, np.int32).T)
    mine = gram(sketch_rows, zc.reshape(1).astype(jnp.int32), table, per, ny * nx, 1.0 / total)
    mine = lax.psum_scatter(mine, ("row", "x"), scatter_dimension=0, tiled=True)
    tiles = lax.all_gather(mine, ("row", "x", "z", "core"), axis=0, tiled=True)

    weights = cross(sketch_rows, theta, nx, 1.0 / math_sqrt(total))
    tiles, weights = lax.optimization_barrier((tiles, weights))
    weights = lax.psum_scatter(weights, "x", scatter_dimension=0, tiled=True)
    weights = lax.psum(weights, "row").reshape(n, width)

    uh, ul, inv = factorize(tiles, n, pairs, per)
    basis, projected = solve(uh, ul, inv, sketch, weights)
    block = n // ny
    return basis, lax.dynamic_slice_in_dim(projected, lax.axis_index("row") * block, block, 0)


def math_sqrt(value):
    return float(np.sqrt(value))


def solution(mesh):
    fine = Mesh(mesh.devices.reshape(4, 4, 4, 2), ("row", "x", "z", "core"))
    col = ("x", "z", "core")
    in_specs = (P("row", col), P("row", col), P(), P(None, "row"))
    out_specs = (P(("row",) + col, None), P("row", col))
    return jax.shard_map(on_device, mesh=fine, in_specs=in_specs, out_specs=out_specs, check_vma=False)
```

time: 1320 us -> 575 us (0.44)
  other arithmetic: 594 us -> 0 us
  matrix products: 205 us -> 0 us
  Pallas kernels: 0 us -> 190 us
  local copies, waits for them, and re-layouts: 91.4 us -> 19.3 us
  waiting for transfers between devices: 365 us -> 323 us
    another operation x77 -> x0, other arithmetic: 579 us -> none  [the longest x7 188 us: right_solve(): jax.scipy.linalg.solve_triangular(lower_block, values.T, lower=True)]
    pallas_call x0 -> x5, Pallas kernels: none -> 190 us  [the longest x1 152 us: factorize(): pl.pallas_call(functools.partial(factor_kernel, pairs, per), out_shape=(j...]
    psum x1, waiting for transfers between devices: 173 us -> 0.02 us  [on_device(): weights = lax.psum(weights, 'row').reshape(n, width)]
    another operation x96 -> x0, matrix products: 115 us -> none  [the longest x66 69.3 us: right_solve(): jax.scipy.linalg.solve_triangular(lower_block, values.T, lower=True)]
    dot_general x21 -> x0, matrix products: 90 us -> none  [the longest x7 37.5 us: exact_dot(): return jnp.dot(first, second, precision=lax.Precision.HIGHEST)]
    all_gather x2 -> x5, waiting for transfers between devices: 73.1 us -> 160 us  [the longest x1 70.2 us: on_device(): tiles = lax.all_gather(mine, ('row', 'x', 'z', 'core'), axis=0, tiled=True)]
    unnamed x5 -> x10, waiting for transfers between devices: 0.75 us -> 75.2 us
    another operation x77 -> x1, local copies, waits for them, and re-layouts: 66.2 us -> 1.05 us  [on_device(): omega_all = lax.all_gather(omega_mine, 'row', axis=0)]
  transfers between devices with their start and end apart: 5 -> 9, of which waited for: 5 -> 8; matrix products, arithmetic and copies ran while one was open for 0% -> 1% of each run, Pallas kernels for 0% -> 27%
where the time goes in v1:
time: 575 us; the launch traced here: 574 us
  waiting for transfers between devices  323 us (56%)
  Pallas kernels  190 us (33%)
  blocking collectives  26.8 us (5%)
  local copies, waits for them, and re-layouts  19.3 us (3%)
  between operations  13.9 us (2%)
    pallas_call x1, Pallas kernels, factorize(): pl.pallas_call(functools.partial(factor_kernel, pairs, per), out_shape=(j...  152 us
    unnamed x10, waiting for transfers between devices  75.2 us
    all_gather x1, waiting for transfers between devices, on_device(): tiles = lax.all_gather(mine, ('row', 'x', 'z', 'core'), axis=0, tiled=True)  70.2 us
    reduce_scatter x1, waiting for transfers between devices, on_device(): weights = lax.psum_scatter(weights, 'x', scatter_dimension=0, tiled=True)  52.7 us
    reduce_scatter x1, waiting for transfers between devices, on_device(): lax.psum_scatter(partial, ('z', 'core'), scatter_dimension=0, tiled=True)  34.7 us
    all_gather x1, waiting for transfers between devices, on_device(): right = lax.all_gather(right, 'x', axis=0)  32.4 us
    all_gather x1, waiting for transfers between devices, on_device(): sketch_rows = lax.all_gather(sketch, ('z', 'core'), axis=0, tiled=True)  26 us
    pallas_call x1, Pallas kernels, solve(): pl.pallas_call(functools.partial(solve_kernel, nt), grid=(nt,), out_shape...  20.9 us
  transfers between devices with their start and end apart: 9, of which 8 were waited for; matrix products, arithmetic and copies ran while one was open for 1% of the time, Pallas kernels for 27%

profile of v1, /device:TPU:0, one launch (start us, length us, event | category | flops | bytes accessed | tf_op | source)
XLA Modules:
  0.0 573.6 jit_solution(211789070539763500)
XLA Ops:
  7.2 0.0 all-gather.8.cloned.1.call-start
  7.2 5.9 %copy.18 = bf16[72,8,32,128]{3,2,1,0:T(8,128)(2,1)} copy(bf16[72,8,32,128]{3,1,2,0:T(8,128)(2,1)} %bitcast.15) | data formatting | bytes 9437184
  13.2 6.2 %dynamic-slice_reduce_fusion = bf16[4,128,576]{1,0,2:T(4,128)(2,1)S(1)} fusion(bf16[4,8,128,576]{2,1,0,3:T(8,128)(2,1)} %bitcast.14, s32[]{:T(128)S(6)} %select_n.6), kind=kLoop, calls=%fused_computation | loop fusion | bytes 1179652 | tf_op jit(solution)/shard_map/dynamic_slice | solution.py:356
  19.3 1.0 all_gather_reshape.3
  20.4 0.0 all-gather.14.cloned.1.call-start
  20.5 0.1 reshape.17
  20.6 10.3 %all_to_all.5 = bf16[4,64,256]{2,1,0:T(8,128)(2,1)} all-to-all(bf16[4,64,256]{2,1,0:T(8,128)(2,1)S(1)} %copy.14), channel_id=1, replica_groups=mesh['row'=4,'x'=4,'z'=4,'core'=2] {'x'}, dimensions={0} | all-to-all | bytes 262144 | tf_op jit(solution)/shard_map/all_to_all | solution.py:351
  30.9 0.0 all-gather.16.cloned.1.call-start
  31.0 16.5 %all_gather.26 = bf16[2048,128]{1,0:T(8,128)(2,1)} all-gather(bf16[512,128]{1,0:T(8,128)(2,1)S(1)} %copy-done), channel_id=1, replica_groups=mesh['row'=4,'x'=4,'z'=4,'core'=2] {'row'}, dimensions={0}, use_global_device_ids=true | all-gather | bytes 655360 | tf_op jit(solution)/shard_map/all_gather | solution.py:353
  47.5 0.0 all-gather.16.cloned.1.call-update
  47.5 0.0 reduce-scatter.6.cloned.1.call-start
  47.6 12.0 %all-gather.8.cloned.1.call-done = bf16[4,512,576]{1,2,0:T(8,128)(2,1)} async-done(((bf16[1,512,576]{1,2,0:T(8,128)(2,1)}), bf16[4,512,576]{1,2,0:T(8,128)(2,1)}) %all-gather.8.cloned.1.call-update) | async-done | bytes 2359312 | tf_op jit(solution)/shard_map/all_gather | solution.py:359
  59.5 4.4 copy.16.omega_ref
  63.9 19.9 %all-gather.14.cloned.1.call-done = bf16[32,64,256]{2,1,0:T(8,128)(2,1)} async-done(((bf16[4,64,256]{2,1,0:T(8,128)(2,1)}), bf16[32,64,256]{2,1,0:T(8,128)(2,1)}) %all-gather.14.cloned.1.call-update) | async-done | bytes 1048592 | tf_op jit(solution)/shard_map/all_gather | solution.py:352
  83.8 32.4 %all-gather.16.cloned.1.call-done = bf16[8192,128]{1,0:T(8,128)(2,1)} async-done(((bf16[2048,128]{1,0:T(8,128)(2,1)}), bf16[8192,128]{1,0:T(8,128)(2,1)}) %all-gather.16.cloned.1.call-update) | async-done | bytes 2097168 | tf_op jit(solution)/shard_map/all_gather | solution.py:354
  116.2 6.6 %front.1 = (bf16[256,512]{1,0:T(8,128)(2,1)}, f32[256,2304]{1,0:T(8,128)}) custom-call(f32[4,4]{1,0:T(4,128)} %gate_ref.1, bf16[8,4,64,256]{3,2,1,0:T(8,128)(2,1)} %bitcast.18, bf16[4,2048,128]{2,1,0:T(8,128)(2,1)} %bitcast.16, bf16[4,512,576]{2,1,0:T(8,128)(2,1)} %copy.16.omega_ref), custom_call_target="tpu_custom_call" | custom-call | tf_op jit(solution)/shard_map/front/pallas_call | solution.py:75
  122.7 0.0 all-gather.10.cloned.1.call-start
  122.8 34.7 %reduce-scatter.6.cloned.1.call-done.s_ref = f32[32,2304]{1,0:T(8,128)} async-done(((f32[256,2304]{1,0:T(8,128)}), f32[32,2304]{1,0:T(8,128)}) %reduce-scatter.6.cloned.1.call-update) | async-done | bytes 294928 | tf_op jit(solution)/shard_map/reduce_scatter | solution.py:362
  157.5 0.0 reduce-scatter.10.cloned.1.call-start
  157.6 26.0 %all-gather.10.cloned.1.call-done.s_ref = f32[256,2304]{1,0:T(8,128)} async-done(((f32[32,2304]{1,0:T(8,128)}), f32[256,2304]{1,0:T(8,128)}) %all-gather.10.cloned.1.call-update) | async-done | bytes 2359312 | tf_op jit(solution)/shard_map/all_gather | solution.py:364
  183.6 5.5 gram.1
  189.0 0.0 all-gather.12.cloned.1.call-start
  189.1 75.0 %reduce-scatter.10.cloned.1.call-done = f32[1,6,16,256]{3,2,1,0:T(8,128)} async-done(((f32[16,6,16,256]{3,2,1,0:T(8,128)}), f32[1,6,16,256]{3,2,1,0:T(8,128)}) %reduce-scatter.10.cloned.1.call-update) | async-done | bytes 98320
  264.1 0.0 reduce-scatter.8.cloned.1.call-start
  264.2 5.2 cross.1
  269.4 70.2 %all-gather.12.cloned.1.call-done.g_ref = f32[128,6,16,256]{3,2,1,0:T(8,128)} async-done(((f32[1,6,16,256]{3,2,1,0:T(8,128)}), f32[128,6,16,256]{3,2,1,0:T(8,128)}) %all-gather.12.cloned.1.call-update) | async-done | bytes 12582928 | tf_op jit(solution)/shard_map/all_gather | solution.py:371
  339.6 0.2 all-reduce.3.cloned.1.call-start
  339.9 52.7 %reduce-scatter.8.cloned.1.call-done = f32[1,2304,128]{2,1,0:T(8,128)} async-done(((f32[4,2304,128]{2,1,0:T(8,128)}), f32[1,2304,128]{2,1,0:T(8,128)}) %reduce-scatter.8.cloned.1.call-update) | async-done | bytes 1179664 | tf_op jit(solution)/shard_map/reduce_scatter | solution.py:375
  392.6 151.8 %factorize.1 = (bf16[2304,2304]{1,0:T(8,128)(2,1)}, bf16[2304,2304]{1,0:T(8,128)(2,1)}, f32[9,256,256]{2,1,0:T(8,128)}) custom-call(f32[128,6,16,256]{3,2,1,0:T(8,128)} %all-gather.12.cloned.1.call-done.g_ref), custom_call_target="tpu_custom_call" | custom-call | flops 24461180928 | bytes 42467328 | tf_op jit(solution)/shard_map/factorize/pallas_call | solution.py:260
  544.5 0.0 all-reduce.3.cloned.1.call-done.w_ref
  544.5 20.9 %solve.1 = (f32[32,2304]{1,0:T(8,128)}, f32[2304,128]{1,0:T(8,128)}) custom-call(bf16[2304,2304]{1,0:T(8,128)(2,1)} %get-tuple-element.14.uh_ref, bf16[2304,2304]{1,0:T(8,128)(2,1)} %get-tuple-element.15.ul_ref, f32[9,256,256]{2,1,0:T(8,128)} %get-tuple-element.16.inv_ref, f32[32,2304]{1,0:T(8,128)} %reduce-scatter.6.cloned.1.call-done.s_ref, ...), custom_call_target="tpu_custom_call" | custom-call | tf_op jit(solution)/shard_map/solve/pallas_call | solution.py:318
  565.4 1.7 constant_dynamic-slice_fusion
  (13 shorter events, 0.2 us)
Async XLA Ops:
  7.2 52.4 %all-gather.8.cloned.1.call-start = ((), (), s32[]{:S(2)}) async-start(), calls=%async_computation.4 | async-start | bytes 2949120 | tf_op jit(solution)/shard_map/all_gather | solution.py:359
  13.2 7.3 %copy-start.1 = (bf16[1024,64]{0,1:T(8,128)(2,1)S(1)}, bf16[1024,64]{0,1:T(8,128)(2,1)}, u32[]{:S(2)}) copy-start(bf16[1024,64]{0,1:T(8,128)(2,1)} %param.5) | copy-start | bytes 393220
  13.2 17.8 %copy-start = (bf16[512,128]{1,0:T(8,128)(2,1)S(1)}, bf16[512,128]{1,0:T(8,128)(2,1)}, u32[]{:S(2)}) copy-start(bf16[512,128]{1,0:T(8,128)(2,1)} %param.6) | copy-start | bytes 393220
  20.4 63.4 %all-gather.14.cloned.1.call-start = ((), (), s32[]{:S(2)}) async-start(), calls=%async_computation.10 | async-start | bytes 1179648 | tf_op jit(solution)/shard_map/all_gather | solution.py:352
  30.9 85.3 %all-gather.16.cloned.1.call-start = ((), (), s32[]{:S(2)}) async-start(), calls=%async_computation.11 | async-start | bytes 2621440 | tf_op jit(solution)/shard_map/all_gather | solution.py:354
  47.5 110.0 %reduce-scatter.6.cloned.1.call-start = ((), (), s32[]{:S(2)}) async-start(), calls=%async_computation.5 | async-start | bytes 2654208 | tf_op jit(solution)/shard_map/reduce_scatter | solution.py:362
  122.7 60.8 %all-gather.10.cloned.1.call-start = ((), (), s32[]{:S(2)}) async-start(), calls=%async_computation.6 | async-start | bytes 2654208 | tf_op jit(solution)/shard_map/all_gather | solution.py:364
  157.5 106.6 %reduce-scatter.10.cloned.1.call-start = ((), (), s32[]{:S(2)}) async-start(), calls=%async_computation.12 | async-start | bytes 1671168
  189.0 150.6 %all-gather.12.cloned.1.call-start = ((), (), s32[]{:S(2)}) async-start(), calls=%async_computation.7 | async-start | bytes 12681216 | tf_op jit(solution)/shard_map/all_gather | solution.py:371
  264.1 128.5 %reduce-scatter.8.cloned.1.call-start = ((), (), s32[]{:S(2)}) async-start(), calls=%async_computation.8 | async-start | bytes 5898240 | tf_op jit(solution)/shard_map/reduce_scatter | solution.py:375
  339.6 204.8 %all-reduce.3.cloned.1.call-start = ((), (), s32[]{:S(2)}) async-start(), calls=%async_computation.9 | async-start | bytes 2359296 | tf_op jit(solution)/shard_map/psum | solution.py:376
Sparse Core Ops, SparseCore 0:
  20.5 38.9 all-gather.7
  61.3 22.5 all-gather.13
  85.5 30.6 all-gather.15
  122.9 34.6 reduce-scatter.5
  159.1 24.4 all-gather.9
  189.2 74.8 reduce-scatter.9
  267.1 72.4 all-gather.11
  342.0 50.5 reduce-scatter.7
  395.0 46.3 all-reduce.2

commit v2 on v1

--- a/solution.py
+++ b/solution.py
@@ -169,56 +169,96 @@
     return done
 
 
-def factor_kernel(
-    pairs, per, g_ref, uh_ref, ul_ref, inv_ref, grid_ref, a_ref, l1_ref, l2_ref, sem
-):
-    blocks, piece, n = grid_ref.shape
-    t_ref = grid_ref.reshape(n, n)
-    nt = n // TILE
-    chunks = TILE // piece
-    groups = g_ref.shape[0] // chunks
-    source = g_ref.reshape(chunks, groups, per, piece, TILE)
-
-    def fetch(at):
-        i, j = pairs[at]
-        return pltpu.make_async_copy(
-            source.at[:, at // per, at % per],
-            grid_ref.at[pl.ds(i * chunks, chunks), :, pl.ds(j * TILE, TILE)],
-            sem.at[min(i, 1)],
-        )
-
-    for at in range(len(pairs)):
-        fetch(at).start()
-    for at in range(len(pairs)):
-        if pairs[at][0] == 0:
-            fetch(at).wait()
-
-    def factor(l_ref):
+def stage_kernel(plan, per, *refs):
+    first, stop, nt, chunks, has_carry, has_tiles = plan
+    refs = list(refs)
+    g_ref = refs.pop(0) if has_tiles else None
+    carry_ref = refs.pop(0) if has_carry else None
+    uh_ref, ul_ref, inv_ref = refs[:3]
+    refs = refs[3:]
+    last = stop == nt
+    out_ref = None if last else refs.pop(0)
+    grid_ref, a_ref, l_ref, uab_ref, sem = refs[:5]
+    extra_ref = refs[5] if has_carry and has_tiles else None
+    m = (nt - first) * TILE
+    size = nt - first
+    count = stop - first
+    t_ref = grid_ref.reshape(m, m)
+    copies = []
+    if has_tiles:
+        groups = g_ref.shape[0] // chunks
+        source = g_ref.reshape(chunks, groups, per, TILE // chunks, TILE)
+        target = grid_ref if extra_ref is None else extra_ref
+        low, high = (first, stop) if not has_carry else (first, nt)
+        for at, (i, j) in enumerate((i, j) for i in range(low, high) for j in range(i, nt)):
+            rows = pl.ds((i - first) * chunks, chunks)
+            cols = pl.ds((j - first) * TILE, TILE)
+            copies.append(
+                pltpu.make_async_copy(
+                    source.at[:, at // per, at % per], target.at[rows, :, cols], sem.at[0]
+                )
+            )
+    if has_carry:
+        for i in range(size):
+            at = pl.ds(i * TILE, TILE)
+            cols = pl.ds(i * TILE, m - i * TILE)
+            copies.append(pltpu.make_async_copy(carry_ref.at[at, cols], t_ref.at[at, cols], sem.at[1]))
+    for copy in copies:
+        copy.start()
+    if not has_carry and not last:
+        t_ref[count * TILE :, count * TILE :] = jnp.zeros((m - count * TILE,) * 2, F32)
+    for copy in copies:
+        copy.wait()
+    if extra_ref is not None:
+        e_ref = extra_ref.reshape(m, m)
+
+        def add_row(r, carry):
+            rat = pl.multiple_of(r * TILE, TILE)
+
+            def add(c, carry):
+                cat = pl.multiple_of(c * TILE, TILE)
+                t_ref[pl.ds(rat, TILE), pl.ds(cat, TILE)] += e_ref[pl.ds(rat, TILE), pl.ds(cat, TILE)]
+                return carry
+
+            return lax.fori_loop(r, size, add, carry)
+
+        lax.fori_loop(0, size, add_row, 0)
+
+    def half(p, h, carry):
+        base = pl.multiple_of(p * TILE, TILE)
+        mid = pl.multiple_of(p * TILE + HALF, HALF)
+
+        @pl.when(h == 0)
+        def _():
+            a_ref[...] = t_ref[pl.ds(base, HALF), pl.ds(base, HALF)]
+
+        @pl.when(h == 1)
+        def _():
+            a_ref[...] = t_ref[pl.ds(mid, HALF), pl.ds(mid, HALF)] - tdot(uab_ref[...], uab_ref[...], HI)
+
         out = leaf([a_ref[8 * i : 8 * i + 8, :] for i in range(HALF // 8)])
         for i, rows in enumerate(out):
             l_ref[8 * i : 8 * i + 8, :] = rows
 
+        @pl.when(h == 0)
+        def _():
+            inv_ref[p, 0:HALF, 0:HALF] = l_ref[...]
+            inv_ref[p, 0:HALF, HALF:] = jnp.zeros((HALF, HALF), F32)
+            uab_ref[...] = jnp.dot(
+                l_ref[...], t_ref[pl.ds(base, HALF), pl.ds(mid, HALF)], precision=HI
+            )
+
+        @pl.when(h == 1)
+        def _():
+            cross = tdot(uab_ref[...], inv_ref[p, 0:HALF, 0:HALF], HI)
+            inv_ref[p, HALF:, 0:HALF] = -jnp.dot(l_ref[...], cross, precision=HI)
+            inv_ref[p, HALF:, HALF:] = l_ref[...]
+
+        return carry
+
     def panel(p, carry):
         base = pl.multiple_of(p * TILE, TILE)
-        mid = pl.multiple_of(p * TILE + HALF, HALF)
-        a_ref[...] = t_ref[pl.ds(base, HALF), pl.ds(base, HALF)]
-        factor(l1_ref)
-        l1 = l1_ref[...]
-        uab = jnp.dot(l1, t_ref[pl.ds(base, HALF), pl.ds(mid, HALF)], precision=HI)
-        a_ref[...] = t_ref[pl.ds(mid, HALF), pl.ds(mid, HALF)] - tdot(uab, uab, HI)
-        factor(l2_ref)
-        l2 = l2_ref[...]
-        l21 = -jnp.dot(l2, tdot(uab, l1, HI), precision=HI)
-        inv_ref[p, 0:HALF, 0:HALF] = l1
-        inv_ref[p, 0:HALF, HALF:] = jnp.zeros((HALF, HALF), F32)
-        inv_ref[p, HALF:, 0:HALF] = l21
-        inv_ref[p, HALF:, HALF:] = l2
-
-        @pl.when(p == 0)
-        def _():
-            for at in range(len(pairs)):
-                if pairs[at][0] != 0:
-                    fetch(at).wait()
+        lax.fori_loop(0, 2, functools.partial(half, p), 0)
 
         def row_tile(c, carry):
             at = pl.multiple_of(c * TILE, TILE)
@@ -228,7 +268,7 @@
             ul_ref[pl.ds(base, TILE), pl.ds(at, TILE)] = rest
             return carry
 
-        lax.fori_loop(p + 1, nt, row_tile, 0)
+        lax.fori_loop(p + 1, size, row_tile, 0)
 
         def trail_row(r, carry):
             rat = pl.multiple_of(r * TILE, TILE)
@@ -246,97 +286,135 @@
                 t_ref[pl.ds(rat, TILE), pl.ds(cat, TILE)] -= update
                 return carry
 
-            lax.fori_loop(r, nt, trail, 0)
+            lax.fori_loop(r, size, trail, 0)
             return carry
 
-        lax.fori_loop(p + 1, nt, trail_row, 0)
+        lax.fori_loop(p + 1, size, trail_row, 0)
         return carry
 
-    lax.fori_loop(0, nt, panel, 0)
-
-
-def factorize(tiles, n, pairs, per):
-    piece = tiles.shape[2]
+    lax.fori_loop(0, count, panel, 0)
+    if out_ref is not None:
+        back = []
+        for i in range(count, size):
+            at = pl.ds((i - count) * TILE, TILE)
+            cols = pl.ds((i - count) * TILE, m - i * TILE)
+            mine = t_ref.at[pl.ds(i * TILE, TILE), pl.ds(i * TILE, m - i * TILE)]
+            back.append(pltpu.make_async_copy(mine, out_ref.at[at, cols], sem.at[0]))
+        for copy in back:
+            copy.start()
+        for copy in back:
+            copy.wait()
+
+
+def stage(first, stop, n, per, chunks, tiles=None, carry=None):
+    nt = n // TILE
+    m = n - first * TILE
+    rows = (stop - first) * TILE
+    piece = TILE // chunks
+    args = [v for v in (tiles, carry) if v is not None]
+    out_shape = [
+        jax.ShapeDtypeStruct((rows, m), BF16),
+        jax.ShapeDtypeStruct((rows, m), BF16),
+        jax.ShapeDtypeStruct((stop - first, TILE, TILE), F32),
+    ]
+    out_specs = [WHOLE] * 3
+    if stop < nt:
+        out_shape.append(jax.ShapeDtypeStruct((m - rows, m - rows), F32))
+        out_specs.append(pl.BlockSpec(memory_space=pl.ANY))
+    scratch = [
+        pltpu.VMEM((m // piece, piece, m), F32),
+        pltpu.VMEM((HALF, HALF), F32),
+        pltpu.VMEM((HALF, HALF), F32),
+        pltpu.VMEM((HALF, HALF), F32),
+        pltpu.SemaphoreType.DMA((2,)),
+    ]
+    if len(args) == 2:
+        scratch.append(pltpu.VMEM((m // piece, piece, m), F32))
+    plan = (first, stop, nt, chunks, carry is not None, tiles is not None)
     return pl.pallas_call(
-        functools.partial(factor_kernel, pairs, per),
-        out_shape=(
-            jax.ShapeDtypeStruct((n, n), BF16),
-            jax.ShapeDtypeStruct((n, n), BF16),
-            jax.ShapeDtypeStruct((n // TILE, TILE, TILE), F32),
-        ),
-        in_specs=[pl.BlockSpec(memory_space=pl.ANY)],
-        out_specs=(WHOLE,) * 3,
-        scratch_shapes=[
-            pltpu.VMEM((n // piece, piece, n), F32),
-            pltpu.VMEM((HALF, HALF), F32),
-            pltpu.VMEM((HALF, HALF), F32),
-            pltpu.VMEM((HALF, HALF), F32),
-            pltpu.SemaphoreType.DMA((2,)),
-        ],
+        functools.partial(stage_kernel, plan, per),
+        out_shape=tuple(out_shape),
+        in_specs=[pl.BlockSpec(memory_space=pl.ANY)] * len(args),
+        out_specs=tuple(out_specs),
+        scratch_shapes=scratch,
         compiler_params=pltpu.CompilerParams(vmem_limit_bytes=VMEM_LIMIT),
         cost_estimate=pl.CostEstimate(
-            flops=2 * n**3, bytes_accessed=n * n * 8, transcendentals=0
+            flops=40 * 10**9, bytes_accessed=rows * m * 8, transcendentals=0
         ),
-        name="factorize",
-    )(tiles)
-
-
-def solve_kernel(nt, uh_ref, ul_ref, inv_ref, s_ref, w_ref, basis_ref, proj_ref, y_ref):
-    p = pl.program_id(0)
+        name=f"stage{first}",
+    )(*args)
+
+
+def solve_kernel(plan, *refs):
+    stages = len(plan)
+    factors = refs[: 3 * stages]
+    s_ref, w_ref, basis_ref, proj_ref, y_ref = refs[3 * stages : 3 * stages + 5]
+    held = refs[3 * stages + 5 : 6 * stages + 5]
+    sem = refs[6 * stages + 5]
+    copies = [
+        pltpu.make_async_copy(a, b, sem.at[q]) for q, (a, b) in enumerate(zip(factors, held))
+    ]
+    for copy in copies:
+        copy.start()
     mine, n = s_ref.shape
-
-    @pl.when(p == 0)
-    def _():
-        padded = jnp.concatenate([s_ref[...], jnp.zeros((HALF - mine, n), F32)], axis=0)
-        y_ref[:, :HALF] = padded.T
-        y_ref[:, HALF:] = w_ref[...]
-
-    base = pl.multiple_of(p * TILE, TILE)
-    y = jnp.dot(inv_ref[0], y_ref[pl.ds(base, TILE), :], precision=HI)
-    y_ref[pl.ds(base, TILE), :] = y
-    proj_ref[pl.ds(base, TILE), :] = y[:, HALF:]
-    head, rest = split(y)
-
-    def tail(r, carry):
-        at = pl.multiple_of(r * TILE, TILE)
-        uh = uh_ref[:, pl.ds(at, TILE)]
-        ul = ul_ref[:, pl.ds(at, TILE)]
-        y_ref[pl.ds(at, TILE), :] -= tdot(uh, head) + (tdot(uh, rest) + tdot(ul, head))
-        return carry
-
-    lax.fori_loop(p + 1, nt, tail, 0)
-
-    @pl.when(p == nt - 1)
-    def _():
-        basis_ref[...] = y_ref[:, :HALF].T[:mine]
-
-
-def solve(uh, ul, inv, sketch, weights):
+    nt = n // TILE
+    padded = jnp.concatenate([s_ref[...], jnp.zeros((HALF - mine, n), F32)], axis=0)
+    y_ref[:, :HALF] = padded.T
+    y_ref[:, HALF:] = w_ref[...]
+    for q, (first, stop) in enumerate(plan):
+        uh_ref, ul_ref, inv_ref = held[3 * q : 3 * q + 3]
+        for copy in copies[3 * q : 3 * q + 3]:
+            copy.wait()
+        for p in range(first, stop):
+            rows = slice(p * TILE, (p + 1) * TILE)
+            local = slice((p - first) * TILE, (p - first + 1) * TILE)
+            y = jnp.dot(inv_ref[p - first], y_ref[rows, :], precision=HI)
+            y_ref[rows, :] = y
+            proj_ref[rows, :] = y[:, HALF:]
+            head, rest = split(y)
+
+            def tail(r, carry):
+                at = pl.multiple_of(r * TILE, TILE)
+                here = pl.multiple_of((r - first) * TILE, TILE)
+                uh = uh_ref[local, pl.ds(here, TILE)]
+                ul = ul_ref[local, pl.ds(here, TILE)]
+                y_ref[pl.ds(at, TILE), :] -= tdot(uh, head) + (tdot(uh, rest) + tdot(ul, head))
+                return carry
+
+            lax.fori_loop(p + 1, nt, tail, 0)
+    basis_ref[...] = y_ref[:, :HALF].T[:mine]
+
+
+def solve(plan, factors, sketch, weights):
     mine, n = sketch.shape
-    nt = n // TILE
-    fixed = lambda p: (0, 0)
+    flat = [v for part in factors for v in part]
     return pl.pallas_call(
-        functools.partial(solve_kernel, nt),
-        grid=(nt,),
+        functools.partial(solve_kernel, plan),
         out_shape=(jax.ShapeDtypeStruct((mine, n), F32), jax.ShapeDtypeStruct((n, HALF), F32)),
-        in_specs=[
-            pl.BlockSpec((TILE, n), lambda p: (p, 0)),
-            pl.BlockSpec((TILE, n), lambda p: (p, 0)),
-            pl.BlockSpec((1, TILE, TILE), lambda p: (p, 0, 0)),
-            pl.BlockSpec((mine, n), fixed),
-            pl.BlockSpec((n, HALF), fixed),
-        ],
-        out_specs=(pl.BlockSpec((mine, n), fixed), pl.BlockSpec((n, HALF), fixed)),
-        scratch_shapes=[pltpu.VMEM((n, 2 * HALF), F32)],
+        in_specs=[pl.BlockSpec(memory_space=pl.ANY)] * len(flat) + [WHOLE, WHOLE],
+        out_specs=(WHOLE, WHOLE),
+        scratch_shapes=[pltpu.VMEM((n, 2 * HALF), F32)]
+        + [pltpu.VMEM(v.shape, v.dtype) for v in flat]
+        + [pltpu.SemaphoreType.DMA((len(flat),))],
         compiler_params=pltpu.CompilerParams(vmem_limit_bytes=VMEM_LIMIT),
         name="solve",
-    )(uh, ul, inv, sketch, weights)
-
-
-def tile_pairs(nt, groups):
-    pairs = [(i, j) for i in range(nt) for j in range(i, nt)]
-    per = -(-len(pairs) // groups)
-    return pairs, per
+    )(*flat, sketch, weights)
+
+
+CUTS = ((0, 3), (3, 6), (6, 9))
+
+
+def tile_table(nt, groups):
+    cut = CUTS[0][1]
+    parts = [
+        [(i, j) for i in range(low, high) for j in range(i, nt)] for low, high in ((0, cut), (cut, nt))
+    ]
+    per = -(-max(len(part) for part in parts) // groups)
+    padded = [part + [(0, 0)] * (per * groups - len(part)) for part in parts]
+    dealt = [
+        padded[half][g * per + t] for g in range(groups) for half in range(2) for t in range(per)
+    ]
+    return np.array(dealt, np.int32).T, per
 
 
 def on_device(left_site, right_site, gate, omega):
@@ -363,20 +441,25 @@
     n = sketch.shape[1]
     sketch_rows = lax.all_gather(sketch, ("z", "core"), axis=0, tiled=True)
 
-    pairs, per = tile_pairs(n // TILE, groups)
-    padded = pairs + [(0, 0)] * (per * groups - len(pairs))
-    table = jnp.asarray(np.array(padded, np.int32).T)
-    mine = gram(sketch_rows, zc.reshape(1).astype(jnp.int32), table, per, ny * nx, 1.0 / total)
-    mine = lax.psum_scatter(mine, ("row", "x"), scatter_dimension=0, tiled=True)
-    tiles = lax.all_gather(mine, ("row", "x", "z", "core"), axis=0, tiled=True)
-
+    table, per = tile_table(n // TILE, groups)
+    group = zc.reshape(1).astype(jnp.int32)
+    chunks = ny * nx
+    mine = gram(sketch_rows, group, jnp.asarray(table), 2 * per, chunks, 1.0 / total)
+    mine = lax.psum_scatter(mine, "row", scatter_dimension=0, tiled=True)
+    mine = lax.psum_scatter(mine, "x", scatter_dimension=0, tiled=True)
+    everywhere = ("row", "x", "z", "core")
+    early = lax.all_gather(mine[:, :per], everywhere, axis=0, tiled=True)
     weights = cross(sketch_rows, theta, nx, 1.0 / math_sqrt(total))
-    tiles, weights = lax.optimization_barrier((tiles, weights))
+    early, late, weights = lax.optimization_barrier((early, mine[:, per:], weights))
+    late = lax.all_gather(late, everywhere, axis=0, tiled=True)
     weights = lax.psum_scatter(weights, "x", scatter_dimension=0, tiled=True)
+
+    *part_a, carry = stage(*CUTS[0], n, per, chunks, tiles=early)
+    *part_b, carry = stage(*CUTS[1], n, per, chunks, tiles=late, carry=carry)
+    carry, weights = lax.optimization_barrier((carry, weights))
     weights = lax.psum(weights, "row").reshape(n, width)
-
-    uh, ul, inv = factorize(tiles, n, pairs, per)
-    basis, projected = solve(uh, ul, inv, sketch, weights)
+    part_c = stage(*CUTS[2], n, per, chunks, carry=carry)
+    basis, projected = solve(CUTS, (part_a, part_b, part_c), sketch, weights)
     block = n // ny
     return basis, lax.dynamic_slice_in_dim(projected, lax.axis_index("row") * block, block, 0)
 

time: 575 us -> 509 us (0.89)
  waiting for transfers between devices: 323 us -> 248 us
  Pallas kernels: 190 us -> 198 us
    unnamed x10 -> x11, waiting for transfers between devices: 75.2 us -> 0.7 us
    reduce_scatter x1, waiting for transfers between devices: 52.7 us -> 0.02 us  [on_device(): weights = lax.psum_scatter(weights, 'x', scatter_dimension=0, tiled=True)]
    reduce_scatter x0 -> x2, waiting for transfers between devices: none -> 49.4 us  [the longest x1 26.3 us: on_device(): mine = lax.psum_scatter(mine, 'row', scatter_dimension=0, tiled=True)]
    psum x1, waiting for transfers between devices: 0.02 us -> 8.92 us  [on_device(): weights = lax.psum(weights, 'row').reshape(n, width)]
    pallas_call x2 -> x4, Pallas kernels: 173 us -> 181 us  [the longest x3 160 us: stage(): pl.pallas_call(functools.partial(stage_kernel, plan, per), out_shape=tupl...]
    all_gather x1 -> x2, waiting for transfers between devices: 70.2 us -> 64.2 us  [the longest x1 64.2 us: on_device(): early = lax.all_gather(mine[:, :per], everywhere, axis=0, tiled=True)]
  transfers between devices with their start and end apart: 9 -> 11, of which waited for: 8 -> 9; matrix products, arithmetic and copies ran while one was open for 1% -> 1% of each run, Pallas kernels for 27% -> 32%
where the time goes in v2:
time: 509 us
  waiting for transfers between devices  248 us (49%)
  Pallas kernels  198 us (39%)
  blocking collectives  26.8 us (5%)
  local copies, waits for them, and re-layouts  20.8 us (4%)
  between operations  14 us (3%)
    pallas_call x3, Pallas kernels, stage(): pl.pallas_call(functools.partial(stage_kernel, plan, per), out_shape=tupl...  160 us
    all_gather x1, waiting for transfers between devices, on_device(): early = lax.all_gather(mine[:, :per], everywhere, axis=0, tiled=True)  64.2 us
    reduce_scatter x1, waiting for transfers between devices, on_device(): lax.psum_scatter(partial, ('z', 'core'), scatter_dimension=0, tiled=True)  34.8 us
    all_gather x1, waiting for transfers between devices, on_device(): right = lax.all_gather(right, 'x', axis=0)  32.4 us
    reduce_scatter x1, waiting for transfers between devices, on_device(): mine = lax.psum_scatter(mine, 'row', scatter_dimension=0, tiled=True)  26.3 us
    all_gather x1, waiting for transfers between devices, on_device(): sketch_rows = lax.all_gather(sketch, ('z', 'core'), axis=0, tiled=True)  26 us
    reduce_scatter x1, waiting for transfers between devices, on_device(): mine = lax.psum_scatter(mine, 'x', scatter_dimension=0, tiled=True)  23.1 us
    pallas_call x1, Pallas kernels, solve(): pl.pallas_call(functools.partial(solve_kernel, plan), out_shape=(jax.Shap...  21.1 us
  transfers between devices with their start and end apart: 11, of which 9 were waited for; matrix products, arithmetic and copies ran while one was open for 1% of the time, Pallas kernels for 32%

profile of v2, /device:TPU:0, one launch (start us, length us, event | category | flops | bytes accessed | tf_op | source)
XLA Modules:
  0.0 508.5 jit_solution(16778890547375111241)
XLA Ops:
  7.2 6.0 %copy.18 = bf16[72,8,32,128]{3,2,1,0:T(8,128)(2,1)} copy(bf16[72,8,32,128]{3,1,2,0:T(8,128)(2,1)} %bitcast.14) | data formatting | bytes 9437184
  13.2 6.2 %dynamic-slice_reduce_fusion = bf16[4,128,576]{1,0,2:T(4,128)(2,1)S(1)} fusion(bf16[4,8,128,576]{2,1,0,3:T(8,128)(2,1)} %bitcast.13, s32[]{:T(128)S(6)} %select_n.6), kind=kLoop, calls=%fused_computation | loop fusion | bytes 1179652 | tf_op jit(solution)/shard_map/dynamic_slice | solution.py:434
  19.4 1.1 all_gather_reshape.3
  20.4 0.0 all-gather.17.cloned.1.call-start
  20.5 0.1 reshape.17
  20.6 10.3 %all_to_all.5 = bf16[4,64,256]{2,1,0:T(8,128)(2,1)} all-to-all(bf16[4,64,256]{2,1,0:T(8,128)(2,1)S(1)} %copy.14), channel_id=1, replica_groups=mesh['row'=4,'x'=4,'z'=4,'core'=2] {'x'}, dimensions={0} | all-to-all | bytes 262144 | tf_op jit(solution)/shard_map/all_to_all | solution.py:429
  30.9 0.0 all-gather.19.cloned.1.call-start
  31.0 16.5 %all_gather.29 = bf16[2048,128]{1,0:T(8,128)(2,1)} all-gather(bf16[512,128]{1,0:T(8,128)(2,1)S(1)} %copy-done), channel_id=1, replica_groups=mesh['row'=4,'x'=4,'z'=4,'core'=2] {'row'}, dimensions={0}, use_global_device_ids=true | all-gather | bytes 655360 | tf_op jit(solution)/shard_map/all_gather | solution.py:431
  47.6 0.0 reduce-scatter.5.cloned.1.call-start
  47.6 12.0 %all-gather.9.cloned.1.call-done = bf16[4,512,576]{1,2,0:T(8,128)(2,1)} async-done(((bf16[1,512,576]{1,2,0:T(8,128)(2,1)}), bf16[4,512,576]{1,2,0:T(8,128)(2,1)}) %all-gather.9.cloned.1.call-update) | async-done | bytes 2359312 | tf_op jit(solution)/shard_map/all_gather | solution.py:437
  59.6 4.3 copy.16.omega_ref
  63.9 19.9 %all-gather.17.cloned.1.call-done = bf16[32,64,256]{2,1,0:T(8,128)(2,1)} async-done(((bf16[4,64,256]{2,1,0:T(8,128)(2,1)}), bf16[32,64,256]{2,1,0:T(8,128)(2,1)}) %all-gather.17.cloned.1.call-update) | async-done | bytes 1048592 | tf_op jit(solution)/shard_map/all_gather | solution.py:430
  83.8 32.4 %all-gather.19.cloned.1.call-done = bf16[8192,128]{1,0:T(8,128)(2,1)} async-done(((bf16[2048,128]{1,0:T(8,128)(2,1)}), bf16[8192,128]{1,0:T(8,128)(2,1)}) %all-gather.19.cloned.1.call-update) | async-done | bytes 2097168 | tf_op jit(solution)/shard_map/all_gather | solution.py:432
  116.2 6.5 %front.1 = (bf16[256,512]{1,0:T(8,128)(2,1)}, f32[256,2304]{1,0:T(8,128)}) custom-call(f32[4,4]{1,0:T(4,128)} %gate_ref.1, bf16[8,4,64,256]{3,2,1,0:T(8,128)(2,1)} %bitcast.17, bf16[4,2048,128]{2,1,0:T(8,128)(2,1)} %bitcast.15, bf16[4,512,576]{2,1,0:T(8,128)(2,1)} %copy.16.omega_ref), custom_call_target="tpu_custom_call" | custom-call | tf_op jit(solution)/shard_map/front/pallas_call | solution.py:75
  122.7 0.0 all-gather.11.cloned.1.call-start
  122.8 34.8 %reduce-scatter.5.cloned.1.call-done.refs_9_ = f32[32,2304]{1,0:T(8,128)} async-done(((f32[256,2304]{1,0:T(8,128)}), f32[32,2304]{1,0:T(8,128)}) %reduce-scatter.5.cloned.1.call-update) | async-done | bytes 294928 | tf_op jit(solution)/shard_map/reduce_scatter | solution.py:440
  157.6 26.0 %all-gather.11.cloned.1.call-done.s_ref = f32[256,2304]{1,0:T(8,128)} async-done(((f32[32,2304]{1,0:T(8,128)}), f32[256,2304]{1,0:T(8,128)}) %all-gather.11.cloned.1.call-update) | async-done | bytes 2359312 | tf_op jit(solution)/shard_map/all_gather | solution.py:442
  183.6 5.4 %gram.1 = f32[16,6,16,256]{3,2,1,0:T(8,128)} custom-call(s32[1]{0:T(128)} %bitcast.group_ref, s32[48]{0:T(128)} %constant.26.i_ref, s32[48]{0:T(128)} %constant.28.j_ref, f32[256,2304]{1,0:T(8,128)} %all-gather.11.cloned.1.call-done.s_ref), custom_call_target="tpu_custom_call" | custom-call | tf_op jit(solution)/shard_map/gram/pallas_call | solution.py:102
  189.0 0.0 reduce-scatter.9.cloned.1.call-start
  189.1 26.3 %reduce-scatter.7.cloned.1.call-done = f32[4,6,16,256]{3,2,1,0:T(8,128)} async-done(((f32[16,6,16,256]{3,2,1,0:T(8,128)}), f32[4,6,16,256]{3,2,1,0:T(8,128)}) %reduce-scatter.7.cloned.1.call-update) | async-done | bytes 393232 | tf_op jit(solution)/shard_map/reduce_scatter | solution.py:448
  215.4 23.1 %reduce-scatter.9.cloned.1.call-done = f32[1,6,16,256]{3,2,1,0:T(8,128)} async-done(((f32[4,6,16,256]{3,2,1,0:T(8,128)}), f32[1,6,16,256]{3,2,1,0:T(8,128)}) %reduce-scatter.9.cloned.1.call-update) | async-done | bytes 98320 | tf_op jit(solution)/shard_map/reduce_scatter | solution.py:449
  238.6 1.5 fusion
  240.1 0.0 all-gather.15.cloned.1.call-start
  240.1 5.3 %cross.1 = f32[4,2304,128]{2,1,0:T(8,128)} custom-call(f32[256,2304]{1,0:T(8,128)} %all-gather.11.cloned.1.call-done.s_ref, bf16[256,512]{1,0:T(8,128)(2,1)} %get-tuple-element.23.theta_ref), custom_call_target="tpu_custom_call" | custom-call | tf_op jit(solution)/shard_map/cross/pallas_call | solution.py:123
  245.4 64.2 %all-gather.13.cloned.1.call-done.refs_0_ = f32[128,3,16,256]{3,2,1,0:T(8,128)} async-done(((f32[1,3,16,256]{3,2,1,0:T(8,128)}), f32[128,3,16,256]{3,2,1,0:T(8,128)}) %all-gather.13.cloned.1.call-update) | async-done | bytes 6291472 | tf_op jit(solution)/shard_map/all_gather | solution.py:451
  309.6 0.5 reduce-scatter.11.cloned.1.call-update
  310.2 71.9 %stage0.1 = (bf16[768,2304]{1,0:T(8,128)(2,1)}, bf16[768,2304]{1,0:T(8,128)(2,1)}, f32[3,256,256]{2,1,0:T(8,128)}, f32[1536,1536]{1,0:T(8,128)}) custom-call(f32[128,3,16,256]{3,2,1,0:T(8,128)} %all-gather.13.cloned.1.call-done.refs_0_), custom_call_target="tpu_custom_call" | custom-call | flops 40000000000 | bytes 14155776 | tf_op jit(solution)/shard_map/stage0/pallas_call | solution.py:334
  382.2 52.8 %stage3.1 = (bf16[768,1536]{1,0:T(8,128)(2,1)}, bf16[768,1536]{1,0:T(8,128)(2,1)}, f32[3,256,256]{2,1,0:T(8,128)}, f32[768,768]{1,0:T(8,128)}) custom-call(f32[128,3,16,256]{3,2,1,0:T(8,128)} %all-gather.15.cloned.1.call-done.refs_0_, f32[1536,1536]{1,0:T(8,128)} %get-tuple-element.29.refs_1_), custom_call_target="tpu_custom_call" | custom-call | flops 40000000000 | bytes 9437184 | tf_op jit(solution)/shard_map/stage3/pallas_call | solution.py:334
  435.0 35.3 %stage6.1 = (bf16[768,768]{1,0:T(8,128)(2,1)}, bf16[768,768]{1,0:T(8,128)(2,1)}, f32[3,256,256]{2,1,0:T(8,128)}) custom-call(f32[768,768]{1,0:T(8,128)} %get-tuple-element.35.refs_0_), custom_call_target="tpu_custom_call" | custom-call | flops 40000000000 | bytes 4718592 | tf_op jit(solution)/shard_map/stage6/pallas_call | solution.py:334
  470.3 8.9 %all-reduce.2.cloned.1.call-done.refs_10_ = f32[2304,128]{1,0:T(8,128)} async-done(((f32[2304,128]{1,0:T(8,128)}), f32[2304,128]{1,0:T(8,128)}) %all-reduce.2.cloned.1.call-update) | async-done | bytes 1179664 | tf_op jit(solution)/shard_map/psum | solution.py:460
  479.2 21.1 %solve.1 = (f32[32,2304]{1,0:T(8,128)}, f32[2304,128]{1,0:T(8,128)}) custom-call(bf16[768,2304]{1,0:T(8,128)(2,1)} %get-tuple-element.25.refs_0_, bf16[768,2304]{1,0:T(8,128)(2,1)} %get-tuple-element.26.refs_1_, f32[3,256,256]{2,1,0:T(8,128)} %get-tuple-element.27.refs_2_, bf16[768,1536]{1,0:T(8,128)(2,1)} %get-tuple-element.30.refs_3_, ...), custom_call_target="tpu_custom_call" | custom-call | tf_op jit(solution)/shard_map/solve/pallas_call | solution.py:391
  500.3 1.7 constant_dynamic-slice_fusion
  (22 shorter events, 0.4 us)
Async XLA Ops:
  7.2 52.4 %all-gather.9.cloned.1.call-start = ((), (), s32[]{:S(2)}) async-start(), calls=%async_computation.5 | async-start | bytes 2949120 | tf_op jit(solution)/shard_map/all_gather | solution.py:437
  13.2 7.3 %copy-start.1 = (bf16[1024,64]{0,1:T(8,128)(2,1)S(1)}, bf16[1024,64]{0,1:T(8,128)(2,1)}, u32[]{:S(2)}) copy-start(bf16[1024,64]{0,1:T(8,128)(2,1)} %param.5) | copy-start | bytes 393220
  13.2 17.8 %copy-start = (bf16[512,128]{1,0:T(8,128)(2,1)S(1)}, bf16[512,128]{1,0:T(8,128)(2,1)}, u32[]{:S(2)}) copy-start(bf16[512,128]{1,0:T(8,128)(2,1)} %param.6) | copy-start | bytes 393220
  20.4 63.4 %all-gather.17.cloned.1.call-start = ((), (), s32[]{:S(2)}) async-start(), calls=%async_computation.14 | async-start | bytes 1179648 | tf_op jit(solution)/shard_map/all_gather | solution.py:430
  30.9 85.3 %all-gather.19.cloned.1.call-start = ((), (), s32[]{:S(2)}) async-start(), calls=%async_computation.15 | async-start | bytes 2621440 | tf_op jit(solution)/shard_map/all_gather | solution.py:432
  47.6 110.0 %reduce-scatter.5.cloned.1.call-start = ((), (), s32[]{:S(2)}) async-start(), calls=%async_computation.6 | async-start | bytes 2654208 | tf_op jit(solution)/shard_map/reduce_scatter | solution.py:440
  122.7 60.8 %all-gather.11.cloned.1.call-start = ((), (), s32[]{:S(2)}) async-start(), calls=%async_computation.7 | async-start | bytes 2654208 | tf_op jit(solution)/shard_map/all_gather | solution.py:442
  157.6 57.8 %reduce-scatter.7.cloned.1.call-start = ((), (), s32[]{:S(2)}) async-start(), calls=%async_computation.8 | async-start | bytes 1966080 | tf_op jit(solution)/shard_map/reduce_scatter | solution.py:448
  189.0 49.5 %reduce-scatter.9.cloned.1.call-start = ((), (), s32[]{:S(2)}) async-start(), calls=%async_computation.9 | async-start | bytes 491520 | tf_op jit(solution)/shard_map/reduce_scatter | solution.py:449
  215.4 94.2 %all-gather.13.cloned.1.call-start = ((), (), s32[]{:S(2)}) async-start(), calls=%async_computation.10 | async-start | bytes 6340608 | tf_op jit(solution)/shard_map/all_gather | solution.py:451
  240.1 142.1 %all-gather.15.cloned.1.call-start = ((), (), s32[]{:S(2)}) async-start(), calls=%async_computation.11 | async-start | bytes 6340608 | tf_op jit(solution)/shard_map/all_gather | solution.py:454
  309.6 125.4 %reduce-scatter.11.cloned.1.call-start = ((), (), s32[]{:S(2)}) async-start(), calls=%async_computation.12 | async-start | bytes 5898240 | tf_op jit(solution)/shard_map/reduce_scatter | solution.py:455
  310.2 169.0 %all-reduce.2.cloned.1.call-start = ((), (), s32[]{:S(2)}) async-start(), calls=%async_computation.13 | async-start | bytes 2359296 | tf_op jit(solution)/shard_map/psum | solution.py:460
Sparse Core Ops, SparseCore 0:
  20.6 38.9 all-gather.8
  61.3 22.5 all-gather.16
  85.5 30.6 all-gather.18
  122.9 34.6 reduce-scatter.4
  159.1 24.4 all-gather.10
  189.2 26.1 reduce-scatter.6
  217.7 20.7 reduce-scatter.8
  241.6 67.9 all-gather.12
  313.1 65.7 all-gather.14
  381.2 48.4 reduce-scatter.10
  435.1 44.0 all-reduce.1

commit v3 on v2

--- a/solution.py
+++ b/solution.py
@@ -28,13 +28,69 @@
     )
 
 
-def front_kernel(gate_ref, left_ref, right_ref, omega_ref, theta_ref, sketch_ref, bond_ref):
-    groups, lanes_x, part, rows = left_ref.shape
-    for xs in range(lanes_x):
-        for zc in range(groups):
-            at = (xs * groups + zc) * part
-            bond_ref[at : at + part, :] = left_ref[zc, xs]
-    width = right_ref.shape[2]
+def around(index, size, step):
+    return lax.rem(index + step, size)
+
+
+def front_kernel(
+    sizes, per, scale, gate_ref, left_ref, right_ref, omega_hbm,
+    theta_ref, rows_ref, mine_ref, tiles_ref,
+    mine_left, all_left, all_right, all_omega, bond_ref,
+    part_ref, pair_ref, sent_ref, got_ref, held_ref, gram_ref, grams_ref,
+    local, o_send, o_recv, r_send, r_recv, l_send, l_recv, g_send, g_recv, pair_send, pair_recv, z_send, z_recv, b_send, b_recv, f_send, f_recv,
+):
+    ny, nx, nz, nc = sizes
+    groups = nz * nc
+    y, x, z, c = (lax.axis_index(a) for a in ("row", "x", "z", "core"))
+    zc = z * nc + c
+    other = 1 - c
+    mesh = pl.DeviceIdType.MESH
+    part, rows = mine_left.shape[1:]
+    bond_y, width = right_ref.shape
+    step = omega_hbm.shape[1]
+
+    def push(src, dst, s, r, to):
+        return pltpu.make_async_remote_copy(
+            src_ref=src, dst_ref=dst, send_sem=s, recv_sem=r, device_id=to, device_id_type=mesh
+        )
+
+    for q in range(nx):
+        mine_left[q] = left_ref[q * rows : (q + 1) * rows, :].T
+    omega_moves, own_moves, right_moves, left_moves = [], [], [], []
+    source = omega_hbm.reshape(nx, groups * width, step)
+    src = source.at[:, pl.ds(pl.multiple_of(zc * width, width), width), :]
+    own_moves.append(pltpu.make_async_copy(src, all_omega.at[y], local))
+    for dy in range(1, ny):
+        to = (around(y, ny, dy), x, z, c)
+        omega_moves.append(push(src, all_omega.at[y], o_send.at[dy - 1], o_recv.at[dy - 1], to))
+    home = all_right.at[x, pl.ds(pl.multiple_of(y * bond_y, bond_y), bond_y), :]
+    for dy in range(ny):
+        for dx in range(nx):
+            if dy or dx:
+                to = (around(y, ny, dy), around(x, nx, dx), z, c)
+                at = len(right_moves)
+                right_moves.append(push(right_ref, home, r_send.at[at], r_recv.at[at], to))
+    for dx in range(nx):
+        to_x = around(x, nx, dx)
+        for dz in range(nz):
+            for dc in range(nc):
+                if dx or dz or dc:
+                    to = (y, to_x, around(z, nz, dz), around(c, nc, dc))
+                    at = len(left_moves)
+                    left_moves.append(
+                        push(mine_left.at[to_x], all_left.at[zc, x], l_send.at[at], l_recv.at[at], to)
+                    )
+    for move in right_moves + left_moves + omega_moves + own_moves:
+        move.start()
+    all_left[zc, x] = mine_left[x]
+    all_right[x, pl.ds(pl.multiple_of(y * bond_y, bond_y), bond_y), :] = right_ref[...]
+    for move in right_moves + left_moves:
+        move.wait_recv()
+
+    for xs in range(nx):
+        for g in range(groups):
+            at = (xs * groups + g) * part
+            bond_ref[at : at + part, :] = all_left[g, xs]
     left = bond_ref[...]
     row_odd = lax.broadcasted_iota(jnp.int32, (rows, width), 0) % 2 == 1
     col_odd = lax.broadcasted_iota(jnp.int32, (rows, width), 1) % 2 == 1
@@ -48,8 +104,8 @@
         odd = jnp.where(col_odd, entry(1, 1), entry(1, 0))
         return jnp.where(row_odd, odd, even)
 
-    for xs in range(right_ref.shape[0]):
-        bare = tdot(left, right_ref[xs])
+    for xs in range(nx):
+        bare = tdot(left, all_right[xs])
         row_partner = jnp.where(row_odd, pltpu.roll(bare, 1, 0), pltpu.roll(bare, rows - 1, 0))
 
         def col_partner(v):
@@ -59,54 +115,151 @@
             coupling(1, 0) * row_partner + coupling(1, 1) * col_partner(row_partner)
         )
         theta_ref[:, xs * width : (xs + 1) * width] = mixed.astype(BF16)
+    for move in own_moves:
+        move.wait()
+    for move in omega_moves:
+        move.wait_recv()
     theta = theta_ref[...]
-    step = omega_ref.shape[2]
-    for y in range(omega_ref.shape[0]):
-        sketch_ref[:, y * step : (y + 1) * step] = jnp.dot(
-            theta, omega_ref[y], preferred_element_type=F32
+    band = rows // groups
+    for q in range(ny):
+        value = jnp.dot(theta, all_omega[q].reshape(nx * width, step), preferred_element_type=F32)
+        part_ref[:, :, q * step : (q + 1) * step] = value.reshape(groups, band, step)
+
+    pair_moves = []
+    for dz in range(1, nz + 1):
+        to_z = around(z, nz, dz)
+        pair_moves.append(
+            push(part_ref.at[to_z * nc + other], pair_ref.at[dz - 1], pair_send.at[dz - 1],
+                 pair_recv.at[dz - 1], (y, x, z, other))
         )
-
-
-def front(gate, left, right, omega):
-    rows = left.shape[3]
-    bond = right.shape[1]
-    cols = right.shape[0] * right.shape[2]
-    k = omega.shape[0] * omega.shape[2]
+    for move in pair_moves:
+        move.start()
+    z_moves = []
+    for dz in range(1, nz):
+        to_z = around(z, nz, dz)
+        pair_moves[dz - 1].wait_recv()
+        sent_ref[dz - 1] = part_ref[to_z * nc + c] + pair_ref[dz - 1]
+        move = push(sent_ref.at[dz - 1], got_ref.at[dz - 1], z_send.at[dz - 1], z_recv.at[dz - 1],
+                    (y, x, to_z, c))
+        move.start()
+        z_moves.append(move)
+    pair_moves[nz - 1].wait_recv()
+    total = part_ref[zc] + pair_ref[nz - 1]
+    for dz in range(1, nz):
+        z_moves[dz - 1].wait_recv()
+        total = total + got_ref[dz - 1]
+    held_ref[zc] = total
+    mine_ref[...] = total
+
+    b_moves, f_moves = [], []
+    for dz in range(1, nz):
+        b_moves.append(
+            push(held_ref.at[zc], held_ref.at[zc], b_send.at[dz - 1], b_recv.at[dz - 1],
+                 (y, x, around(z, nz, dz), c))
+        )
+    for dz in range(nz):
+        slot = around(z, nz, nz - dz) * nc + c
+        f_moves.append(
+            push(held_ref.at[slot], held_ref.at[slot], f_send.at[dz], f_recv.at[dz], (y, x, z, other))
+        )
+    for move in b_moves:
+        move.start()
+    f_moves[0].start()
+    for dz in range(1, nz):
+        b_moves[dz - 1].wait_recv()
+        f_moves[dz].start()
+    for move in f_moves:
+        move.wait_recv()
+    rows_ref[...] = held_ref[...].reshape(rows, rows_ref.shape[1])
+
+    chunks, count, piece = gram_ref.shape[:3]
+
+    nt = rows_ref.shape[1] // TILE
+
+    for half, (low, high) in enumerate(tile_halves(nt)):
+        starts = [0]
+        for i in range(low, high):
+            starts.append(starts[-1] + nt - i)
+
+        def tile(t, carry, half=half, low=low, starts=starts):
+            at = jnp.minimum(zc * per + t, starts[-1] - 1)
+            row, begin = jnp.int32(low), jnp.int32(0)
+            for q in range(1, len(starts) - 1):
+                row = jnp.where(at >= starts[q], low + q, row)
+                begin = jnp.where(at >= starts[q], starts[q], begin)
+            i = pl.multiple_of(row * TILE, TILE)
+            j = pl.multiple_of((row + at - begin) * TILE, TILE)
+            value = tdot(rows_ref[:, pl.ds(i, TILE)], rows_ref[:, pl.ds(j, TILE)], HI) * scale
+            gram_ref[:, pl.ds(half * per + t, 1)] = value.reshape(chunks, 1, piece, TILE)
+            return carry
+
+        lax.fori_loop(0, per, tile, 0)
+    me = y * nx + x
+    gram_moves = []
+    for dy in range(ny):
+        for dx in range(nx):
+            if dy or dx:
+                to_y, to_x = around(y, ny, dy), around(x, nx, dx)
+                at = len(gram_moves)
+                gram_moves.append(
+                    push(gram_ref.at[to_y * nx + to_x], grams_ref.at[me], g_send.at[at],
+                         g_recv.at[at], (to_y, to_x, z, c))
+                )
+    for move in gram_moves:
+        move.start()
+    grams_ref[me] = gram_ref[me]
+    for move in gram_moves:
+        move.wait_recv()
+    value = grams_ref[0]
+    for q in range(1, chunks):
+        value = value + grams_ref[q]
+    tiles_ref[...] = value
+    for move in (omega_moves + right_moves + left_moves + pair_moves + z_moves + b_moves + f_moves
+                 + gram_moves):
+        move.wait_send()
+
+
+def front(gate, left, right, omega, sizes, per, scale):
+    ny, nx, nz, nc = sizes
+    groups, chunks = nz * nc, ny * nx
+    rows, part = left.shape[0] // nx, left.shape[1]
+    bond_y, width = right.shape
+    step = omega.shape[1]
+    k, cols, band = ny * step, nx * width, rows // groups
+    piece, count = TILE // chunks, 2 * per
+    smem = pl.BlockSpec(memory_space=pltpu.SMEM)
+    dma = pltpu.SemaphoreType.DMA
     return pl.pallas_call(
-        front_kernel,
-        out_shape=(jax.ShapeDtypeStruct((rows, cols), BF16), jax.ShapeDtypeStruct((rows, k), F32)),
-        in_specs=[pl.BlockSpec(memory_space=pltpu.SMEM), WHOLE, WHOLE, WHOLE],
-        out_specs=(WHOLE, WHOLE),
-        scratch_shapes=[pltpu.VMEM((bond, rows), BF16)],
-        compiler_params=pltpu.CompilerParams(vmem_limit_bytes=VMEM_LIMIT),
+        functools.partial(front_kernel, sizes, per, scale),
+        out_shape=(
+            jax.ShapeDtypeStruct((rows, cols), BF16),
+            jax.ShapeDtypeStruct((rows, k), F32),
+            jax.ShapeDtypeStruct((band, k), F32),
+            jax.ShapeDtypeStruct((count, piece, TILE), F32),
+        ),
+        in_specs=[smem, WHOLE, WHOLE, pl.BlockSpec(memory_space=pl.ANY)],
+        out_specs=(WHOLE,) * 4,
+        scratch_shapes=[
+            pltpu.VMEM((nx, part, rows), BF16),
+            pltpu.VMEM((groups, nx, part, rows), BF16),
+            pltpu.VMEM((nx, bond_y * ny, width), BF16),
+            pltpu.VMEM((ny, nx, width, step), BF16),
+            pltpu.VMEM((bond_y * ny, rows), BF16),
+            pltpu.VMEM((groups, band, k), F32),
+            pltpu.VMEM((nz, band, k), F32),
+            pltpu.VMEM((nz - 1, band, k), F32),
+            pltpu.VMEM((nz - 1, band, k), F32),
+            pltpu.VMEM((groups, band, k), F32),
+            pltpu.VMEM((chunks, count, piece, TILE), F32),
+            pltpu.VMEM((chunks, count, piece, TILE), F32),
+            dma, dma((ny - 1,)), dma((ny - 1,)), dma((chunks - 1,)), dma((chunks - 1,)),
+            dma((nx * groups - 1,)), dma((nx * groups - 1,)), dma((chunks - 1,)), dma((chunks - 1,)),
+            dma((nz,)), dma((nz,)), dma((nz - 1,)), dma((nz - 1,)),
+            dma((nz - 1,)), dma((nz - 1,)), dma((nz,)), dma((nz,)),
+        ],
+        compiler_params=pltpu.CompilerParams(vmem_limit_bytes=VMEM_LIMIT, has_side_effects=True),
         name="front",
     )(gate, left, right, omega)
-
-
-def gram_kernel(scale, per, group_ref, i_ref, j_ref, s_ref, out_ref):
-    chunks, piece = out_ref.shape[0], out_ref.shape[2]
-
-    def tile(t, carry):
-        at = group_ref[0] * per + t
-        i = pl.multiple_of(i_ref[at] * TILE, TILE)
-        j = pl.multiple_of(j_ref[at] * TILE, TILE)
-        value = tdot(s_ref[:, pl.ds(i, TILE)], s_ref[:, pl.ds(j, TILE)], HI) * scale
-        out_ref[:, pl.ds(t, 1)] = value.reshape(chunks, 1, piece, TILE)
-        return carry
-
-    lax.fori_loop(0, per, tile, 0)
-
-
-def gram(sketch, group, pairs, per, chunks, scale):
-    smem = pl.BlockSpec(memory_space=pltpu.SMEM)
-    return pl.pallas_call(
-        functools.partial(gram_kernel, scale, per),
-        out_shape=jax.ShapeDtypeStruct((chunks, per, TILE // chunks, TILE), F32),
-        in_specs=[smem, smem, smem, WHOLE],
-        out_specs=WHOLE,
-        compiler_params=pltpu.CompilerParams(vmem_limit_bytes=VMEM_LIMIT),
-        name="gram",
-    )(group, pairs[0], pairs[1], sketch)
 
 
 def cross_kernel(scale, s_ref, theta_ref, out_ref):
@@ -404,49 +557,28 @@
 CUTS = ((0, 3), (3, 6), (6, 9))
 
 
-def tile_table(nt, groups):
+def tile_halves(nt):
     cut = CUTS[0][1]
-    parts = [
-        [(i, j) for i in range(low, high) for j in range(i, nt)] for low, high in ((0, cut), (cut, nt))
-    ]
-    per = -(-max(len(part) for part in parts) // groups)
-    padded = [part + [(0, 0)] * (per * groups - len(part)) for part in parts]
-    dealt = [
-        padded[half][g * per + t] for g in range(groups) for half in range(2) for t in range(per)
-    ]
-    return np.array(dealt, np.int32).T, per
+    return (0, cut), (cut, nt)
+
+
+def tiles_each(nt, groups):
+    counts = [sum(nt - i for i in range(low, high)) for low, high in tile_halves(nt)]
+    return -(-max(counts) // groups)
 
 
 def on_device(left_site, right_site, gate, omega):
-    ny, nx, nz, nc = (lax.axis_size(a) for a in ("row", "x", "z", "core"))
-    groups = nz * nc
-    rows_y, part = left_site.shape
-    rows = rows_y // nx
-    total = rows_y * ny
-    zc = lax.axis_index("z") * nc + lax.axis_index("core")
-
-    left = left_site.T.reshape(part, nx, rows).transpose(1, 0, 2)
-    left = lax.all_to_all(left, "x", 0, 0)
-    left = lax.all_gather(left, ("z", "core"), axis=0)
-    right = lax.all_gather(right_site, "row", axis=0, tiled=True)
-    right = lax.all_gather(right, "x", axis=0)
+    sizes = tuple(lax.axis_size(a) for a in ("row", "x", "z", "core"))
+    ny, nx, nz, nc = sizes
+    total = left_site.shape[0] * ny
     width = right_site.shape[1]
-    omega_mine = lax.dynamic_slice_in_dim(
-        omega.reshape(nx, groups, width, omega.shape[1]), zc, 1, 1
-    ).reshape(nx * width, omega.shape[1])
-    omega_all = lax.all_gather(omega_mine, "row", axis=0)
-
-    theta, partial = front(gate, left, right, omega_all)
-    sketch = lax.psum_scatter(partial, ("z", "core"), scatter_dimension=0, tiled=True)
-    n = sketch.shape[1]
-    sketch_rows = lax.all_gather(sketch, ("z", "core"), axis=0, tiled=True)
-
-    table, per = tile_table(n // TILE, groups)
-    group = zc.reshape(1).astype(jnp.int32)
+    n = omega.shape[1] * ny
     chunks = ny * nx
-    mine = gram(sketch_rows, group, jnp.asarray(table), 2 * per, chunks, 1.0 / total)
-    mine = lax.psum_scatter(mine, "row", scatter_dimension=0, tiled=True)
-    mine = lax.psum_scatter(mine, "x", scatter_dimension=0, tiled=True)
+    per = tiles_each(n // TILE, nz * nc)
+    theta, sketch_rows, sketch, mine = front(
+        gate, left_site, right_site, omega, sizes, per, 1.0 / total
+    )
+    mine = mine[None]
     everywhere = ("row", "x", "z", "core")
     early = lax.all_gather(mine[:, :per], everywhere, axis=0, tiled=True)
     weights = cross(sketch_rows, theta, nx, 1.0 / math_sqrt(total))

time: 509 us -> 418 us (0.82)
  waiting for transfers between devices: 248 us -> 71.9 us
  Pallas kernels: 198 us -> 319 us
  blocking collectives: 26.8 us -> 0 us
  local copies, waits for them, and re-layouts: 20.8 us -> 12.5 us
    pallas_call x2 -> x1, Pallas kernels: 12 us -> 133 us  [front(): pl.pallas_call(functools.partial(front_kernel, sizes, per, scale), out_sh...]
    all_gather x4 -> x0, waiting for transfers between devices: 90.2 us -> none  [the longest x1 32.4 us: on_device(): right = lax.all_gather(right, 'x', axis=0)]
    reduce_scatter x3 -> x0, waiting for transfers between devices: 84.2 us -> none  [the longest x1 34.8 us: on_device(): lax.psum_scatter(partial, ('z', 'core'), scatter_dimension=0, tiled=True)]
    all_gather x1 -> x0, blocking collectives: 16.5 us -> none  [on_device(): right = lax.all_gather(right_site, 'row', axis=0, tiled=True)]
    all_to_all x1 -> x0, blocking collectives: 10.3 us -> none  [on_device(): left = lax.all_to_all(left, 'x', 0, 0)]
    dynamic_slice x1 -> x0, local copies, waits for them, and re-layouts: 6.18 us -> none  [on_device(): lax.dynamic_slice_in_dim(omega.reshape(nx, groups, width, omega.shape[1])...]
  transfers between devices with their start and end apart: 11 -> 4, of which waited for: 9 -> 2; matrix products, arithmetic and copies ran while one was open for 1% -> 0% of each run, Pallas kernels for 32% -> 40%
where the time goes in v3:
time: 418 us
  Pallas kernels  319 us (76%)
  waiting for transfers between devices  71.9 us (17%)
  between operations  13.8 us (3%)
  local copies, waits for them, and re-layouts  12.5 us (3%)
    pallas_call x3, Pallas kernels, stage(): pl.pallas_call(functools.partial(stage_kernel, plan, per), out_shape=tupl...  160 us
    pallas_call x1, Pallas kernels, front(): pl.pallas_call(functools.partial(front_kernel, sizes, per, scale), out_sh...  133 us
    all_gather x1, waiting for transfers between devices, on_device(): early = lax.all_gather(mine[:, :per], everywhere, axis=0, tiled=True)  61.9 us
    pallas_call x1, Pallas kernels, solve(): pl.pallas_call(functools.partial(solve_kernel, plan), out_shape=(jax.Shap...  21.1 us
    unnamed x2, local copies, waits for them, and re-layouts  9.35 us
    psum x1, waiting for transfers between devices, on_device(): weights = lax.psum(weights, 'row').reshape(n, width)  9.25 us
  transfers between devices with their start and end apart: 4, of which 2 were waited for; matrix products, arithmetic and copies ran while one was open for 0% of the time, Pallas kernels for 40%

profile of v3, /device:TPU:0, one launch (start us, length us, event | category | flops | bytes accessed | tf_op | source)
XLA Modules:
  0.0 417.8 jit_solution(3266738841301266775)
XLA Ops:
  7.2 0.0 all-gather.3.cloned.1.call-start
  7.2 1.7 copy.8.left_ref
  9.0 7.6 %copy.9.omega_hbm = bf16[4096,576]{1,0:T(8,128)(2,1)} copy(bf16[4096,576]{0,1:T(8,128)(2,1)} %param.7) | data formatting | bytes 9437184 | tf_op args[3]
  16.6 133.0 %front.1 = (bf16[256,512]{1,0:T(8,128)(2,1)}, f32[256,2304]{1,0:T(8,128)}, f32[32,2304]{1,0:T(8,128)}, f32[6,16,256]{2,1,0:T(8,128)}) custom-call(f32[4,4]{1,0:T(4,128)} %gate_ref.1, bf16[1024,64]{1,0:T(8,128)(2,1)} %copy.8.left_ref, bf16[512,128]{1,0:T(8,128)(2,1)} %right_ref.1, bf16[4096,576]{1,0:T(8,128)(2,1)} %copy.9.omega_hbm), custom_call_target="tpu_custom_call" | custom-call | tf_op jit(solution)/shard_map/front/pallas_call | solution.py:232
  149.5 1.5 fusion
  151.0 0.0 all-gather.3.cloned.1.call-update
  151.0 0.0 all-gather.5.cloned.1.call-start
  151.1 5.2 %cross.1 = f32[4,2304,128]{2,1,0:T(8,128)} custom-call(f32[256,2304]{1,0:T(8,128)} %get-tuple-element.25.s_ref, bf16[256,512]{1,0:T(8,128)(2,1)} %get-tuple-element.26.theta_ref), custom_call_target="tpu_custom_call" | custom-call | tf_op jit(solution)/shard_map/cross/pallas_call | solution.py:276
  156.3 61.9 %all-gather.3.cloned.1.call-done.refs_0_ = f32[128,3,16,256]{3,2,1,0:T(8,128)} async-done(((f32[1,3,16,256]{3,2,1,0:T(8,128)}), f32[128,3,16,256]{3,2,1,0:T(8,128)}) %all-gather.3.cloned.1.call-update) | async-done | bytes 6291472 | tf_op jit(solution)/shard_map/all_gather | solution.py:583
  218.2 0.0 all-gather.5.cloned.1.call-update
  218.2 0.0 reduce-scatter.2.cloned.1.call-start
  218.3 0.7 reduce-scatter.2.cloned.1.call-update
  219.0 0.0 all-reduce.2.cloned.1.call-start
  219.0 72.0 %stage0.1 = (bf16[768,2304]{1,0:T(8,128)(2,1)}, bf16[768,2304]{1,0:T(8,128)(2,1)}, f32[3,256,256]{2,1,0:T(8,128)}, f32[1536,1536]{1,0:T(8,128)}) custom-call(f32[128,3,16,256]{3,2,1,0:T(8,128)} %all-gather.3.cloned.1.call-done.refs_0_), custom_call_target="tpu_custom_call" | custom-call | flops 40000000000 | bytes 14155776 | tf_op jit(solution)/shard_map/stage0/pallas_call | solution.py:487
  291.0 0.0 all-gather.5.cloned.1.call-done.refs_0_
  291.0 52.8 %stage3.1 = (bf16[768,1536]{1,0:T(8,128)(2,1)}, bf16[768,1536]{1,0:T(8,128)(2,1)}, f32[3,256,256]{2,1,0:T(8,128)}, f32[768,768]{1,0:T(8,128)}) custom-call(f32[128,3,16,256]{3,2,1,0:T(8,128)} %all-gather.5.cloned.1.call-done.refs_0_, f32[1536,1536]{1,0:T(8,128)} %get-tuple-element.32.refs_1_), custom_call_target="tpu_custom_call" | custom-call | flops 40000000000 | bytes 9437184 | tf_op jit(solution)/shard_map/stage3/pallas_call | solution.py:487
  343.9 0.0 reduce-scatter.2.cloned.1.call-done
  343.9 0.0 all-reduce.2.cloned.1.call-update
  343.9 35.3 %stage6.1 = (bf16[768,768]{1,0:T(8,128)(2,1)}, bf16[768,768]{1,0:T(8,128)(2,1)}, f32[3,256,256]{2,1,0:T(8,128)}) custom-call(f32[768,768]{1,0:T(8,128)} %get-tuple-element.38.refs_0_), custom_call_target="tpu_custom_call" | custom-call | flops 40000000000 | bytes 4718592 | tf_op jit(solution)/shard_map/stage6/pallas_call | solution.py:487
  379.2 9.2 %all-reduce.2.cloned.1.call-done.refs_10_ = f32[2304,128]{1,0:T(8,128)} async-done(((f32[2304,128]{1,0:T(8,128)}), f32[2304,128]{1,0:T(8,128)}) %all-reduce.2.cloned.1.call-update) | async-done | bytes 1179664 | tf_op jit(solution)/shard_map/psum | solution.py:592
  388.4 21.1 %solve.1 = (f32[32,2304]{1,0:T(8,128)}, f32[2304,128]{1,0:T(8,128)}) custom-call(bf16[768,2304]{1,0:T(8,128)(2,1)} %get-tuple-element.28.refs_0_, bf16[768,2304]{1,0:T(8,128)(2,1)} %get-tuple-element.29.refs_1_, f32[3,256,256]{2,1,0:T(8,128)} %get-tuple-element.30.refs_2_, bf16[768,1536]{1,0:T(8,128)(2,1)} %get-tuple-element.33.refs_3_, ...), custom_call_target="tpu_custom_call" | custom-call | tf_op jit(solution)/shard_map/solve/pallas_call | solution.py:544
  409.5 1.7 constant_dynamic-slice_fusion
Async XLA Ops:
  7.2 211.1 %all-gather.3.cloned.1.call-start = ((), (), s32[]{:S(2)}) async-start(), calls=%async_computation.1 | async-start | bytes 6340608 | tf_op jit(solution)/shard_map/all_gather | solution.py:583
  151.0 140.0 %all-gather.5.cloned.1.call-start = ((), (), s32[]{:S(2)}) async-start(), calls=%async_computation.2 | async-start | bytes 6340608 | tf_op jit(solution)/shard_map/all_gather | solution.py:586
  218.2 125.6 %reduce-scatter.2.cloned.1.call-start = ((), (), s32[]{:S(2)}) async-start(), calls=%async_computation.3 | async-start | bytes 5898240 | tf_op jit(solution)/shard_map/reduce_scatter | solution.py:587
  219.0 169.4 %all-reduce.2.cloned.1.call-start = ((), (), s32[]{:S(2)}) async-start(), calls=%async_computation.4 | async-start | bytes 2359296 | tf_op jit(solution)/shard_map/psum | solution.py:592
Sparse Core Ops, SparseCore 0:
  151.1 67.0 all-gather.2
  221.8 65.7 all-gather.4
  290.0 48.5 reduce-scatter.1
  344.0 44.3 all-reduce.1

commit v4 on v2

--- a/solution.py
+++ b/solution.py
@@ -28,13 +28,156 @@
     )
 
 
-def front_kernel(gate_ref, left_ref, right_ref, omega_ref, theta_ref, sketch_ref, bond_ref):
-    groups, lanes_x, part, rows = left_ref.shape
-    for xs in range(lanes_x):
-        for zc in range(groups):
-            at = (xs * groups + zc) * part
-            bond_ref[at : at + part, :] = left_ref[zc, xs]
-    width = right_ref.shape[2]
+def near(index, size, step):
+    return lax.rem(index + (step + size), size)
+
+
+def front_kernel(
+    sizes, per, scale, cross_scale, gate_ref, left_ref, right_ref, omega_hbm,
+    mine_ref, early_ref, late_ref, cross_ref,
+    theta_ref, all_left, all_right, all_omega, bond_ref,
+    part_ref, pair_ref, relay_ref, got_ref, held_ref,
+    ya_ref, ya_relay, ya_got, xa_ref, xa_relay, xa_got,
+    xb_ref, xb_relay, xb_got, yb_ref, yb_relay, yb_got,
+    local, send, recv,
+):
+    ny, nx, nz, nc = sizes
+    groups = nz * nc
+    y, x, z, c = (lax.axis_index(a) for a in ("row", "x", "z", "core"))
+    zc = z * nc + c
+    twin = (y, x, z, 1 - c)
+    part = left_ref.shape[0]
+    rows = all_left.shape[3]
+    bond_y, width = right_ref.shape
+    step = omega_hbm.shape[0]
+    band = rows // groups
+    moves = []
+
+    def push(src, dst, to):
+        at = len(moves)
+        move = pltpu.make_async_remote_copy(
+            src_ref=src, dst_ref=dst, send_sem=send.at[at], recv_sem=recv.at[at],
+            device_id=to, device_id_type=pl.DeviceIdType.MESH,
+        )
+        moves.append(move)
+        return move
+
+    def beside(axis, way):
+        place = [y, x, z, c]
+        place[axis] = near(place[axis], sizes[axis], way)
+        return tuple(place)
+
+    class Gather:
+        def __init__(self, axis, block):
+            me = (y, x, z)[axis]
+            self.below, self.above = near(me, 4, -1), near(me, 4, 1)
+            up, down = beside(axis, 1), beside(axis, -1)
+            own = block(me, None)
+            self.up, self.down = push(own, own, up), push(own, own, down)
+            first, second = block(self.below, 0), block(self.above, 1)
+            self.far_up, self.far_down = push(first, first, up), push(second, second, down)
+
+        def start(self):
+            self.up.start()
+            self.down.start()
+
+        def relay(self):
+            self.up.wait_recv()
+            self.far_up.start()
+            self.down.wait_recv()
+            self.far_down.start()
+
+        def finish(self):
+            self.far_up.wait_recv()
+            self.far_down.wait_recv()
+
+    class Reduce:
+        def __init__(self, axis, block, relay, got):
+            me = (y, x, z)[axis]
+            up, down = beside(axis, 1), beside(axis, -1)
+            far, above, below = near(me, 4, 2), near(me, 4, 1), near(me, 4, -1)
+            self.block, self.me, self.above, self.below, self.far = block, me, above, below, far
+            self.relay, self.got = relay, got
+            self.far_up = push(block(far, 0), relay.at[0], up)
+            self.far_down = push(block(far, 1), relay.at[1], down)
+            self.up = push(block(above, None), got.at[0], up)
+            self.down = push(block(below, None), got.at[1], down)
+
+        def start(self):
+            self.far_up.start()
+            self.far_down.start()
+
+        def middle(self):
+            self.far_up.wait_recv()
+            self.block(self.above, 0)[...] += self.relay[0]
+            self.up.start()
+            self.far_down.wait_recv()
+            self.block(self.below, 1)[...] += self.relay[1]
+            self.down.start()
+
+        def finish(self):
+            self.up.wait_recv()
+            self.down.wait_recv()
+            return self.block(self.me, None)[...] + self.got[0] + self.got[1]
+
+    def halved(ref, rows_of, half):
+        return ref if half is None else ref.at[pl.ds(half * (rows_of // 2), rows_of // 2)]
+
+    def right_y(slot, half):
+        size = bond_y if half is None else bond_y // 2
+        begin = slot * bond_y + (0 if half is None else half * size)
+        return all_right.at[x, pl.ds(pl.multiple_of(begin, 128), size), :]
+
+    own_omega = [
+        pltpu.make_async_copy(
+            omega_hbm.at[:, pl.ds(pl.multiple_of((q * groups + zc) * width, width), width)],
+            all_omega.at[y, :, pl.ds(q * width, width)], local.at[q],
+        )
+        for q in range(nx)
+    ]
+    for move in own_omega:
+        move.start()
+    all_right[x, pl.ds(pl.multiple_of(y * bond_y, bond_y), bond_y), :] = right_ref[...]
+    by_y = Gather(0, right_y)
+    by_y.start()
+    across = []
+    for dx in range(1, nx):
+        to_x = near(x, nx, dx)
+        src = left_ref.at[:, pl.ds(pl.multiple_of(to_x * rows, rows), rows)]
+        across.append(push(src, all_left.at[zc, x], (y, to_x, z, c)))
+    for move in across:
+        move.start()
+    all_left[zc, x] = left_ref[:, pl.ds(pl.multiple_of(x * rows, rows), rows)]
+    for move in own_omega:
+        move.wait()
+    omega_y = Gather(0, lambda slot, half: halved(all_omega.at[slot], step, half))
+    omega_y.start()
+    by_y.relay()
+    for move in across:
+        move.wait_recv()
+    left_z = Gather(2, lambda slot, half: halved(all_left.at[slot * nc + c], nx, half))
+    left_z.start()
+    left_twin = [push(all_left.at[near(z, nz, d) * nc + c], all_left.at[near(z, nz, d) * nc + c], twin)
+                 for d in (0, -1, 1, 2)]
+    left_twin[0].start()
+    by_y.finish()
+    by_x = Gather(1, lambda slot, half: halved(all_right.at[slot], bond_y * ny, half))
+    by_x.start()
+    left_z.relay()
+    left_twin[1].start()
+    left_twin[2].start()
+    omega_y.relay()
+    left_z.finish()
+    left_twin[3].start()
+    by_x.relay()
+    for move in left_twin:
+        move.wait_recv()
+    for xs in range(nx):
+        for g in range(groups):
+            at = (xs * groups + g) * part
+            bond_ref[at : at + part, :] = all_left[g, xs]
+    by_x.finish()
+
     left = bond_ref[...]
     row_odd = lax.broadcasted_iota(jnp.int32, (rows, width), 0) % 2 == 1
     col_odd = lax.broadcasted_iota(jnp.int32, (rows, width), 1) % 2 == 1
@@ -48,8 +191,8 @@
         odd = jnp.where(col_odd, entry(1, 1), entry(1, 0))
         return jnp.where(row_odd, odd, even)
 
-    for xs in range(right_ref.shape[0]):
-        bare = tdot(left, right_ref[xs])
+    for xs in range(nx):
+        bare = tdot(left, all_right[xs])
         row_partner = jnp.where(row_odd, pltpu.roll(bare, 1, 0), pltpu.roll(bare, rows - 1, 0))
 
         def col_partner(v):
@@ -59,75 +202,227 @@
             coupling(1, 0) * row_partner + coupling(1, 1) * col_partner(row_partner)
         )
         theta_ref[:, xs * width : (xs + 1) * width] = mixed.astype(BF16)
+    omega_y.finish()
     theta = theta_ref[...]
-    step = omega_ref.shape[2]
-    for y in range(omega_ref.shape[0]):
-        sketch_ref[:, y * step : (y + 1) * step] = jnp.dot(
-            theta, omega_ref[y], preferred_element_type=F32
+    for q in range(ny):
+        value = lax.dot_general(
+            theta, all_omega[q], (((1,), (1,)), ((), ())), preferred_element_type=F32
         )
-
-
-def front(gate, left, right, omega):
-    rows = left.shape[3]
-    bond = right.shape[1]
-    cols = right.shape[0] * right.shape[2]
-    k = omega.shape[0] * omega.shape[2]
+        part_ref[:, :, q * step : (q + 1) * step] = value.reshape(groups, band, step)
+
+    order = (2, 1, -1, 0)
+    pairs = [
+        push(part_ref.at[near(z, nz, d) * nc + 1 - c], pair_ref.at[q], twin) for q, d in enumerate(order)
+    ]
+    for move in pairs:
+        move.start()
+
+    def block_z(slot, half):
+        return halved(part_ref.at[slot * nc + c], band, half)
+
+    def add_pair(q):
+        pairs[q].wait_recv()
+        part_ref[near(z, nz, order[q]) * nc + c] += pair_ref[q]
+
+    sum_z = Reduce(2, block_z, relay_ref, got_ref)
+    add_pair(0)
+    sum_z.start()
+    add_pair(1)
+    add_pair(2)
+    sum_z.middle()
+    add_pair(3)
+    total = sum_z.finish()
+    held_ref[zc] = total
+
+    rows_z = Gather(2, lambda slot, half: halved(held_ref.at[slot * nc + c], band, half))
+    rows_z.start()
+    rows_twin = [push(held_ref.at[near(z, nz, d) * nc + c], held_ref.at[near(z, nz, d) * nc + c], twin)
+                 for d in (0, -1, 1, 2)]
+    rows_twin[0].start()
+    mine_ref[...] = total
+    rows_z.relay()
+    rows_twin[1].start()
+    rows_twin[2].start()
+    rows_z.finish()
+    rows_twin[3].start()
+    for move in rows_twin:
+        move.wait_recv()
+    k = mine_ref.shape[1]
+    nt = k // TILE
+    piece = early_ref.shape[5]
+
+    def columns(at, count=TILE):
+        return held_ref[:, :, pl.ds(at, count)].reshape(rows, count)
+
+    def tiles(half, out):
+        low, high = tile_halves(nt)[half]
+        starts = [0]
+        for i in range(low, high):
+            starts.append(starts[-1] + nt - i)
+
+        def tile(t, carry):
+            at = jnp.minimum(zc * per + t, starts[-1] - 1)
+            row, begin = jnp.int32(low), jnp.int32(0)
+            for q in range(1, len(starts) - 1):
+                row = jnp.where(at >= starts[q], low + q, row)
+                begin = jnp.where(at >= starts[q], starts[q], begin)
+            i = pl.multiple_of(row * TILE, TILE)
+            j = pl.multiple_of((row + at - begin) * TILE, TILE)
+            value = tdot(columns(i), columns(j), HI) * scale
+            for q in range(ny):
+                for r in range(nx):
+                    at = (q * nx + r) * piece
+                    spot = (q, r) if half == 0 else (r, q)
+                    out[spot[0], spot[1], pl.ds(t, 1)] = value[at : at + piece].reshape(1, piece, TILE)
+            return carry
+
+        lax.fori_loop(0, per, tile, 0)
+
+    def lower_rows(ref, slot, half):
+        if half is None:
+            return ref.at[slot]
+        return ref.at[slot, :, pl.ds(half * (piece // 2), piece // 2)]
+
+    first_a = Reduce(0, lambda s, h: halved(ya_ref.at[s], nx, h), ya_relay, ya_got)
+    first_b = Reduce(1, lambda s, h: halved(xb_ref.at[s], ny, h), xb_relay, xb_got)
+    tiles(0, ya_ref)
+    first_a.start()
+    tiles(1, xb_ref)
+    first_a.middle()
+    first_b.start()
+    xa_ref[...] = first_a.finish()
+    then_a = Reduce(1, lambda s, h: lower_rows(xa_ref, s, h), xa_relay, xa_got)
+    then_a.start()
+    first_b.middle()
+    then_a.middle()
+    yb_ref[...] = first_b.finish()
+    then_b = Reduce(0, lambda s, h: lower_rows(yb_ref, s, h), yb_relay, yb_got)
+    then_b.start()
+    early_ref[y, x, z, c] = then_a.finish()
+
+    spots = ((2, 0, 1), (0, 1, 2), (1, 2, 0))
+    here = (y, x, z)
+
+    def plane(t, phase):
+        axes = spots[t]
+        along = axes[phase]
+
+        def block(slot, half):
+            index = [here[0], here[1], here[2]]
+            for done in axes[:phase]:
+                index[done] = slice(None)
+            index[along] = slot
+            if half is not None and phase == 0:
+                rows_at = pl.ds(half * (piece // 2), piece // 2)
+                return early_ref.at[index[0], index[1], index[2], c, t, rows_at]
+            if half is not None:
+                index[axes[0]] = pl.ds(2 * half, 2)
+            return early_ref.at[index[0], index[1], index[2], c, t]
+
+        return along, block
+
+    rings = []
+    for t in range(per):
+        along, block = plane(t, 0)
+        rings.append(Gather(along, block))
+        rings[t].start()
+    then_b.middle()
+    for ring in rings:
+        ring.relay()
+    late_ref[...] = then_b.finish()
+    second = []
+    for t in range(per):
+        rings[t].finish()
+        along, block = plane(t, 1)
+        second.append(Gather(along, block))
+        second[t].start()
+    for ring in second:
+        ring.relay()
+    third, to_twin = [], []
+    for t in range(per):
+        second[t].finish()
+        along, block = plane(t, 2)
+        third.append(Gather(along, block))
+        third[t].start()
+        me = here[along]
+        group = []
+        for d in (0, -1, 1, 2):
+            ref = block(near(me, 4, d), None)
+            group.append(push(ref, ref, twin))
+        to_twin.append(group)
+        group[0].start()
+
+    theta = theta_ref[...]
+    for at in range(0, k, TILE):
+        head, rest = split(columns(at))
+        value = (tdot(head, theta) + tdot(rest, theta)) * cross_scale
+        for q in range(nx):
+            cross_ref[q, at : at + TILE, :] = value[:, q * width : (q + 1) * width]
+
+    for t in range(per):
+        third[t].relay()
+        to_twin[t][1].start()
+        to_twin[t][2].start()
+    for t in range(per):
+        third[t].finish()
+        to_twin[t][3].start()
+    for group in to_twin:
+        for move in group:
+            move.wait_recv()
+    for move in moves:
+        move.wait_send()
+
+
+def front(gate, left, right, omega, sizes, per, scale, cross_scale):
+    ny, nx, nz, nc = sizes
+    groups, chunks = nz * nc, ny * nx
+    part, rows = left.shape[0], left.shape[1] // nx
+    bond_y, width = right.shape
+    step = omega.shape[0]
+    k, cols, band = ny * step, nx * width, rows // groups
+    piece = TILE // chunks
+    smem = pl.BlockSpec(memory_space=pltpu.SMEM)
+    dma = pltpu.SemaphoreType.DMA
+    vmem = pltpu.VMEM
+
+    def sums(first, second):
+        return [
+            vmem((first, second, per, piece, TILE), F32),
+            vmem((2, second // 2, per, piece, TILE), F32),
+            vmem((2, second, per, piece, TILE), F32),
+            vmem((second, per, piece, TILE), F32),
+            vmem((2, per, piece // 2, TILE), F32),
+            vmem((2, per, piece, TILE), F32),
+        ]
+
     return pl.pallas_call(
-        front_kernel,
-        out_shape=(jax.ShapeDtypeStruct((rows, cols), BF16), jax.ShapeDtypeStruct((rows, k), F32)),
-        in_specs=[pl.BlockSpec(memory_space=pltpu.SMEM), WHOLE, WHOLE, WHOLE],
-        out_specs=(WHOLE, WHOLE),
-        scratch_shapes=[pltpu.VMEM((bond, rows), BF16)],
-        compiler_params=pltpu.CompilerParams(vmem_limit_bytes=VMEM_LIMIT),
+        functools.partial(front_kernel, sizes, per, scale, cross_scale),
+        out_shape=(
+            jax.ShapeDtypeStruct((band, k), F32),
+            jax.ShapeDtypeStruct((ny, nx, nz, nc, per, piece, TILE), F32),
+            jax.ShapeDtypeStruct((per, piece, TILE), F32),
+            jax.ShapeDtypeStruct((nx, k, width), F32),
+        ),
+        in_specs=[smem, WHOLE, WHOLE, pl.BlockSpec(memory_space=pl.ANY)],
+        out_specs=(WHOLE,) * 4,
+        scratch_shapes=[
+            vmem((rows, cols), BF16),
+            vmem((groups, nx, part, rows), BF16),
+            vmem((nx, bond_y * ny, width), BF16),
+            vmem((ny, step, cols), BF16),
+            vmem((bond_y * ny, rows), BF16),
+            vmem((groups, band, k), F32),
+            vmem((nz, band, k), F32),
+            vmem((2, band // 2, k), F32),
+            vmem((2, band, k), F32),
+            vmem((groups, band, k), F32),
+        ]
+        + sums(ny, nx)
+        + sums(nx, ny)
+        + [dma((nx,)), dma((128,)), dma((128,))],
+        compiler_params=pltpu.CompilerParams(vmem_limit_bytes=VMEM_LIMIT, has_side_effects=True),
         name="front",
     )(gate, left, right, omega)
-
-
-def gram_kernel(scale, per, group_ref, i_ref, j_ref, s_ref, out_ref):
-    chunks, piece = out_ref.shape[0], out_ref.shape[2]
-
-    def tile(t, carry):
-        at = group_ref[0] * per + t
-        i = pl.multiple_of(i_ref[at] * TILE, TILE)
-        j = pl.multiple_of(j_ref[at] * TILE, TILE)
-        value = tdot(s_ref[:, pl.ds(i, TILE)], s_ref[:, pl.ds(j, TILE)], HI) * scale
-        out_ref[:, pl.ds(t, 1)] = value.reshape(chunks, 1, piece, TILE)
-        return carry
-
-    lax.fori_loop(0, per, tile, 0)
-
-
-def gram(sketch, group, pairs, per, chunks, scale):
-    smem = pl.BlockSpec(memory_space=pltpu.SMEM)
-    return pl.pallas_call(
-        functools.partial(gram_kernel, scale, per),
-        out_shape=jax.ShapeDtypeStruct((chunks, per, TILE // chunks, TILE), F32),
-        in_specs=[smem, smem, smem, WHOLE],
-        out_specs=WHOLE,
-        compiler_params=pltpu.CompilerParams(vmem_limit_bytes=VMEM_LIMIT),
-        name="gram",
-    )(group, pairs[0], pairs[1], sketch)
-
-
-def cross_kernel(scale, s_ref, theta_ref, out_ref):
-    parts, _, width = out_ref.shape
-    for at in range(0, s_ref.shape[1], TILE):
-        head, rest = split(s_ref[:, at : at + TILE])
-        value = (tdot(head, theta_ref[...]) + tdot(rest, theta_ref[...])) * scale
-        for x in range(parts):
-            out_ref[x, at : at + TILE, :] = value[:, x * width : (x + 1) * width]
-
-
-def cross(sketch, theta, parts, scale):
-    width = theta.shape[1] // parts
-    return pl.pallas_call(
-        functools.partial(cross_kernel, scale),
-        out_shape=jax.ShapeDtypeStruct((parts, sketch.shape[1], width), F32),
-        in_specs=[WHOLE, WHOLE],
-        out_specs=WHOLE,
-        compiler_params=pltpu.CompilerParams(vmem_limit_bytes=VMEM_LIMIT),
-        name="cross",
-    )(sketch, theta)
 
 
 def leaf(rows):
@@ -404,54 +699,29 @@
 CUTS = ((0, 3), (3, 6), (6, 9))
 
 
-def tile_table(nt, groups):
+def tile_halves(nt):
     cut = CUTS[0][1]
-    parts = [
-        [(i, j) for i in range(low, high) for j in range(i, nt)] for low, high in ((0, cut), (cut, nt))
-    ]
-    per = -(-max(len(part) for part in parts) // groups)
-    padded = [part + [(0, 0)] * (per * groups - len(part)) for part in parts]
-    dealt = [
-        padded[half][g * per + t] for g in range(groups) for half in range(2) for t in range(per)
-    ]
-    return np.array(dealt, np.int32).T, per
+    return (0, cut), (cut, nt)
+
+
+def tiles_each(nt, groups):
+    counts = [sum(nt - i for i in range(low, high)) for low, high in tile_halves(nt)]
+    return -(-max(counts) // groups)
 
 
 def on_device(left_site, right_site, gate, omega):
-    ny, nx, nz, nc = (lax.axis_size(a) for a in ("row", "x", "z", "core"))
-    groups = nz * nc
-    rows_y, part = left_site.shape
-    rows = rows_y // nx
-    total = rows_y * ny
-    zc = lax.axis_index("z") * nc + lax.axis_index("core")
-
-    left = left_site.T.reshape(part, nx, rows).transpose(1, 0, 2)
-    left = lax.all_to_all(left, "x", 0, 0)
-    left = lax.all_gather(left, ("z", "core"), axis=0)
-    right = lax.all_gather(right_site, "row", axis=0, tiled=True)
-    right = lax.all_gather(right, "x", axis=0)
+    sizes = tuple(lax.axis_size(a) for a in ("row", "x", "z", "core"))
+    ny, nx, nz, nc = sizes
+    total = left_site.shape[0] * ny
     width = right_site.shape[1]
-    omega_mine = lax.dynamic_slice_in_dim(
-        omega.reshape(nx, groups, width, omega.shape[1]), zc, 1, 1
-    ).reshape(nx * width, omega.shape[1])
-    omega_all = lax.all_gather(omega_mine, "row", axis=0)
-
-    theta, partial = front(gate, left, right, omega_all)
-    sketch = lax.psum_scatter(partial, ("z", "core"), scatter_dimension=0, tiled=True)
-    n = sketch.shape[1]
-    sketch_rows = lax.all_gather(sketch, ("z", "core"), axis=0, tiled=True)
-
-    table, per = tile_table(n // TILE, groups)
-    group = zc.reshape(1).astype(jnp.int32)
+    n = omega.shape[1] * ny
     chunks = ny * nx
-    mine = gram(sketch_rows, group, jnp.asarray(table), 2 * per, chunks, 1.0 / total)
-    mine = lax.psum_scatter(mine, "row", scatter_dimension=0, tiled=True)
-    mine = lax.psum_scatter(mine, "x", scatter_dimension=0, tiled=True)
-    everywhere = ("row", "x", "z", "core")
-    early = lax.all_gather(mine[:, :per], everywhere, axis=0, tiled=True)
-    weights = cross(sketch_rows, theta, nx, 1.0 / math_sqrt(total))
-    early, late, weights = lax.optimization_barrier((early, mine[:, per:], weights))
-    late = lax.all_gather(late, everywhere, axis=0, tiled=True)
+    per = tiles_each(n // TILE, nz * nc)
+    sketch, early, late, weights = front(
+        gate, left_site.T, right_site, omega.T, sizes, per, 1.0 / total, 1.0 / math_sqrt(total)
+    )
+    early = early.reshape((ny * nx * nz * nc,) + early.shape[4:])
+    late = lax.all_gather(late[None], ("row", "x", "z", "core"), axis=0, tiled=True)
     weights = lax.psum_scatter(weights, "x", scatter_dimension=0, tiled=True)
 
     *part_a, carry = stage(*CUTS[0], n, per, chunks, tiles=early)

time: 509 us -> 371 us (0.73)
  waiting for transfers between devices: 248 us -> 31.1 us
  Pallas kernels: 198 us -> 322 us
  blocking collectives: 26.8 us -> 0 us
  local copies, waits for them, and re-layouts: 20.8 us -> 1.7 us
    all_gather x6 -> x1, waiting for transfers between devices: 154 us -> 21.2 us  [on_device(): lax.all_gather(late[None], ('row', 'x', 'z', 'core'), axis=0, tiled=True)]
    pallas_call x3 -> x1, Pallas kernels: 17.2 us -> 141 us  [front(): pl.pallas_call(functools.partial(front_kernel, sizes, per, scale, cross_s...]
    reduce_scatter x3 -> x0, waiting for transfers between devices: 84.2 us -> none  [the longest x1 34.8 us: on_device(): lax.psum_scatter(partial, ('z', 'core'), scatter_dimension=0, tiled=True)]
    all_gather x1 -> x0, blocking collectives: 16.5 us -> none  [on_device(): right = lax.all_gather(right_site, 'row', axis=0, tiled=True)]
    all_to_all x1 -> x0, blocking collectives: 10.3 us -> none  [on_device(): left = lax.all_to_all(left, 'x', 0, 0)]
    dynamic_slice x1 -> x0, local copies, waits for them, and re-layouts: 6.18 us -> none  [on_device(): lax.dynamic_slice_in_dim(omega.reshape(nx, groups, width, omega.shape[1])...]
    unnamed x5 -> x0, local copies, waits for them, and re-layouts: 5.96 us -> none
  transfers between devices with their start and end apart: 11 -> 3, of which waited for: 9 -> 2; matrix products, arithmetic and copies ran while one was open for 1% -> 0% of each run, Pallas kernels for 32% -> 43%
where the time goes in v4:
time: 371 us
  Pallas kernels  322 us (87%)
  waiting for transfers between devices  31.1 us (8%)
  between operations  15.5 us (4%)
    pallas_call x3, Pallas kernels, stage(): pl.pallas_call(functools.partial(stage_kernel, plan, per), out_shape=tupl...  160 us
    pallas_call x1, Pallas kernels, front(): pl.pallas_call(functools.partial(front_kernel, sizes, per, scale, cross_s...  141 us
    all_gather x1, waiting for transfers between devices, on_device(): lax.all_gather(late[None], ('row', 'x', 'z', 'core'), axis=0, tiled=True)  21.2 us
    pallas_call x1, Pallas kernels, solve(): pl.pallas_call(functools.partial(solve_kernel, plan), out_shape=(jax.Shap...  21.1 us
    psum x1, waiting for transfers between devices, on_device(): weights = lax.psum(weights, 'row').reshape(n, width)  9.3 us
  transfers between devices with their start and end apart: 3, of which 2 were waited for; matrix products, arithmetic and copies ran while one was open for 0% of the time, Pallas kernels for 43%

profile of v4, /device:TPU:0, one launch (start us, length us, event | category | flops | bytes accessed | tf_op | source)
XLA Modules:
  0.0 370.6 jit_solution(15189920306437896846)
XLA Ops:
  8.0 0.0 all-gather.3.cloned.1.call-start
  8.0 141.1 %front.1 = (f32[32,2304]{1,0:T(8,128)}, f32[4,4,4,2,3,16,256]{6,5,4,3,2,1,0:T(8,128)}, f32[3,16,256]{2,1,0:T(8,128)}, f32[4,2304,128]{2,1,0:T(8,128)}) custom-call(f32[4,4]{1,0:T(4,128)} %gate_ref.1, bf16[64,1024]{1,0:T(8,128)(2,1)} %bitcast.7, bf16[512,128]{1,0:T(8,128)(2,1)} %right_ref.1, bf16[576,4096]{1,0:T(8,128)(2,1)} %bitcast.5), custom_call_target="tpu_custom_call" | custom-call | tf_op jit(solution)/shard_map/front/pallas_call | solution.py:398
  149.2 0.0 all-gather.3.cloned.1.call-update
  149.2 0.0 reduce-scatter.2.cloned.1.call-start
  149.2 0.5 reduce-scatter.2.cloned.1.call-update
  149.8 0.0 all-reduce.2.cloned.1.call-start
  149.8 71.9 %stage0.1 = (bf16[768,2304]{1,0:T(8,128)(2,1)}, bf16[768,2304]{1,0:T(8,128)(2,1)}, f32[3,256,256]{2,1,0:T(8,128)}, f32[1536,1536]{1,0:T(8,128)}) custom-call(f32[128,3,16,256]{3,2,1,0:T(8,128)} %bitcast.9), custom_call_target="tpu_custom_call" | custom-call | flops 40000000000 | bytes 14155776 | tf_op jit(solution)/shard_map/stage0/pallas_call | solution.py:629
  221.7 21.2 %all-gather.3.cloned.1.call-done = f32[384,16,256]{2,1,0:T(8,128)} async-done(((f32[3,16,256]{2,1,0:T(8,128)}), f32[384,16,256]{2,1,0:T(8,128)}) %all-gather.3.cloned.1.call-update) | async-done | bytes 6291472 | tf_op jit(solution)/shard_map/all_gather | solution.py:724
  243.0 52.8 %stage3.1 = (bf16[768,1536]{1,0:T(8,128)(2,1)}, bf16[768,1536]{1,0:T(8,128)(2,1)}, f32[3,256,256]{2,1,0:T(8,128)}, f32[768,768]{1,0:T(8,128)}) custom-call(f32[128,3,16,256]{3,2,1,0:T(8,128)} %bitcast.8, f32[1536,1536]{1,0:T(8,128)} %get-tuple-element.26.refs_1_), custom_call_target="tpu_custom_call" | custom-call | flops 40000000000 | bytes 9437184 | tf_op jit(solution)/shard_map/stage3/pallas_call | solution.py:629
  295.7 0.0 reduce-scatter.2.cloned.1.call-done
  295.8 0.0 all-reduce.2.cloned.1.call-update
  295.8 35.3 %stage6.1 = (bf16[768,768]{1,0:T(8,128)(2,1)}, bf16[768,768]{1,0:T(8,128)(2,1)}, f32[3,256,256]{2,1,0:T(8,128)}) custom-call(f32[768,768]{1,0:T(8,128)} %get-tuple-element.32.refs_0_), custom_call_target="tpu_custom_call" | custom-call | flops 40000000000 | bytes 4718592 | tf_op jit(solution)/shard_map/stage6/pallas_call | solution.py:629
  331.1 9.3 %all-reduce.2.cloned.1.call-done.refs_10_ = f32[2304,128]{1,0:T(8,128)} async-done(((f32[2304,128]{1,0:T(8,128)}), f32[2304,128]{1,0:T(8,128)}) %all-reduce.2.cloned.1.call-update) | async-done | bytes 1179664 | tf_op jit(solution)/shard_map/psum | solution.py:730
  340.4 21.1 %solve.1 = (f32[32,2304]{1,0:T(8,128)}, f32[2304,128]{1,0:T(8,128)}) custom-call(bf16[768,2304]{1,0:T(8,128)(2,1)} %get-tuple-element.22.refs_0_, bf16[768,2304]{1,0:T(8,128)(2,1)} %get-tuple-element.23.refs_1_, f32[3,256,256]{2,1,0:T(8,128)} %get-tuple-element.24.refs_2_, bf16[768,1536]{1,0:T(8,128)(2,1)} %get-tuple-element.27.refs_3_, ...), custom_call_target="tpu_custom_call" | custom-call | tf_op jit(solution)/shard_map/solve/pallas_call | solution.py:686
  361.5 1.7 constant_dynamic-slice_fusion
Async XLA Ops:
  8.0 235.0 %all-gather.3.cloned.1.call-start = ((), (), s32[]{:S(2)}) async-start(), calls=%async_computation.3 | async-start | bytes 6340608 | tf_op jit(solution)/shard_map/all_gather | solution.py:724
  149.2 146.6 %reduce-scatter.2.cloned.1.call-start = ((), (), s32[]{:S(2)}) async-start(), calls=%async_computation.1 | async-start | bytes 5898240 | tf_op jit(solution)/shard_map/reduce_scatter | solution.py:725
  149.8 190.6 %all-reduce.2.cloned.1.call-start = ((), (), s32[]{:S(2)}) async-start(), calls=%async_computation.2 | async-start | bytes 2359296 | tf_op jit(solution)/shard_map/psum | solution.py:730
Sparse Core Ops, SparseCore 0:
  149.3 93.6 all-gather.2
Sparse Core Ops, SparseCore 1:
  152.1 49.2 reduce-scatter.1
  295.9 44.4 all-reduce.1

commit v5 on v4

--- a/solution.py
+++ b/solution.py
@@ -148,11 +148,30 @@
     for move in across:
         move.start()
     all_left[zc, x] = left_ref[:, pl.ds(pl.multiple_of(x * rows, rows), rows)]
+
+    def right_x(row):
+        at = pl.ds(pl.multiple_of(row * bond_y, bond_y), bond_y)
+
+        def block(slot, half):
+            if half is None:
+                return all_right.at[slot, at, :]
+            size = bond_y // 2
+            return all_right.at[slot, pl.ds(pl.multiple_of(row * bond_y + half * size, size), size), :]
+
+        return Gather(1, block)
+
+    by_x = [right_x(near(y, ny, d)) for d in (0, -1, 1, 2)]
+    by_x[0].start()
+    by_y.up.wait_recv()
+    by_y.far_up.start()
+    by_x[1].start()
+    by_y.down.wait_recv()
+    by_y.far_down.start()
+    by_x[2].start()
     for move in own_omega:
         move.wait()
     omega_y = Gather(0, lambda slot, half: halved(all_omega.at[slot], step, half))
     omega_y.start()
-    by_y.relay()
     for move in across:
         move.wait_recv()
     left_z = Gather(2, lambda slot, half: halved(all_left.at[slot * nc + c], nx, half))
@@ -160,23 +179,26 @@
     left_twin = [push(all_left.at[near(z, nz, d) * nc + c], all_left.at[near(z, nz, d) * nc + c], twin)
                  for d in (0, -1, 1, 2)]
     left_twin[0].start()
+    by_x[0].relay()
     by_y.finish()
-    by_x = Gather(1, lambda slot, half: halved(all_right.at[slot], bond_y * ny, half))
-    by_x.start()
+    by_x[3].start()
     left_z.relay()
     left_twin[1].start()
     left_twin[2].start()
-    omega_y.relay()
+    by_x[1].relay()
+    by_x[2].relay()
     left_z.finish()
     left_twin[3].start()
-    by_x.relay()
+    by_x[3].relay()
+    omega_y.relay()
     for move in left_twin:
         move.wait_recv()
     for xs in range(nx):
         for g in range(groups):
             at = (xs * groups + g) * part
             bond_ref[at : at + part, :] = all_left[g, xs]
-    by_x.finish()
+    for ring in by_x:
+        ring.finish()
 
     left = bond_ref[...]
     row_odd = lax.broadcasted_iota(jnp.int32, (rows, width), 0) % 2 == 1
@@ -722,9 +744,10 @@
     )
     early = early.reshape((ny * nx * nz * nc,) + early.shape[4:])
     late = lax.all_gather(late[None], ("row", "x", "z", "core"), axis=0, tiled=True)
+
+    *part_a, carry = stage(*CUTS[0], n, per, chunks, tiles=early)
+    carry, weights = lax.optimization_barrier((carry, weights))
     weights = lax.psum_scatter(weights, "x", scatter_dimension=0, tiled=True)
-
-    *part_a, carry = stage(*CUTS[0], n, per, chunks, tiles=early)
     *part_b, carry = stage(*CUTS[1], n, per, chunks, tiles=late, carry=carry)
     carry, weights = lax.optimization_barrier((carry, weights))
     weights = lax.psum(weights, "row").reshape(n, width)

time: 371 us -> 337 us (0.908)
  waiting for transfers between devices: 31.1 us -> 9.71 us
  Pallas kernels: 322 us -> 310 us
    all_gather x1, waiting for transfers between devices: 21.2 us -> 0.02 us  [on_device(): lax.all_gather(late[None], ('row', 'x', 'z', 'core'), axis=0, tiled=True)]
    pallas_call x1, Pallas kernels: 141 us -> 129 us  [front(): pl.pallas_call(functools.partial(front_kernel, sizes, per, scale, cross_s...]
  transfers between devices with their start and end apart: 3 -> 3, of which waited for: 2 -> 1; matrix products, arithmetic and copies ran while one was open for 0% -> 0% of each run, Pallas kernels for 43% -> 47%
where the time goes in v5:
time: 337 us
  Pallas kernels  310 us (92%)
  between operations  15.5 us (5%)
  waiting for transfers between devices  9.71 us (3%)
    pallas_call x3, Pallas kernels, stage(): pl.pallas_call(functools.partial(stage_kernel, plan, per), out_shape=tupl...  160 us
    pallas_call x1, Pallas kernels, front(): pl.pallas_call(functools.partial(front_kernel, sizes, per, scale, cross_s...  129 us
    pallas_call x1, Pallas kernels, solve(): pl.pallas_call(functools.partial(solve_kernel, plan), out_shape=(jax.Shap...  20.9 us
    psum x1, waiting for transfers between devices, on_device(): weights = lax.psum(weights, 'row').reshape(n, width)  9.61 us
  transfers between devices with their start and end apart: 3, of which 1 were waited for; matrix products, arithmetic and copies ran while one was open for 0% of the time, Pallas kernels for 47%

profile of v5, /device:TPU:0, one launch (start us, length us, event | category | flops | bytes accessed | tf_op | source)
XLA Modules:
  0.0 337.1 jit_solution(10005969616542240006)
XLA Ops:
  8.0 0.0 all-gather.3.cloned.1.call-start
  8.0 129.0 %front.1 = (f32[32,2304]{1,0:T(8,128)}, f32[4,4,4,2,3,16,256]{6,5,4,3,2,1,0:T(8,128)}, f32[3,16,256]{2,1,0:T(8,128)}, f32[4,2304,128]{2,1,0:T(8,128)}) custom-call(f32[4,4]{1,0:T(4,128)} %gate_ref.1, bf16[64,1024]{1,0:T(8,128)(2,1)} %bitcast.7, bf16[512,128]{1,0:T(8,128)(2,1)} %right_ref.1, bf16[576,4096]{1,0:T(8,128)(2,1)} %bitcast.5), custom_call_target="tpu_custom_call" | custom-call | tf_op jit(solution)/shard_map/front/pallas_call | solution.py:420
  137.0 0.0 all-gather.3.cloned.1.call-update
  137.1 0.0 reduce-scatter.2.cloned.1.call-start
  137.1 71.9 %stage0.1 = (bf16[768,2304]{1,0:T(8,128)(2,1)}, bf16[768,2304]{1,0:T(8,128)(2,1)}, f32[3,256,256]{2,1,0:T(8,128)}, f32[1536,1536]{1,0:T(8,128)}) custom-call(f32[128,3,16,256]{3,2,1,0:T(8,128)} %bitcast.9), custom_call_target="tpu_custom_call" | custom-call | flops 40000000000 | bytes 14155776 | tf_op jit(solution)/shard_map/stage0/pallas_call | solution.py:651
  209.1 0.0 reduce-scatter.2.cloned.1.call-update
  209.1 0.2 all-reduce.2.cloned.1.call-start
  209.3 0.0 all-gather.3.cloned.1.call-done
  209.3 52.8 %stage3.1 = (bf16[768,1536]{1,0:T(8,128)(2,1)}, bf16[768,1536]{1,0:T(8,128)(2,1)}, f32[3,256,256]{2,1,0:T(8,128)}, f32[768,768]{1,0:T(8,128)}) custom-call(f32[128,3,16,256]{3,2,1,0:T(8,128)} %bitcast.8, f32[1536,1536]{1,0:T(8,128)} %get-tuple-element.30.refs_1_), custom_call_target="tpu_custom_call" | custom-call | flops 40000000000 | bytes 9437184 | tf_op jit(solution)/shard_map/stage3/pallas_call | solution.py:651
  262.1 0.0 reduce-scatter.2.cloned.1.call-done
  262.1 0.0 all-reduce.2.cloned.1.call-update
  262.2 35.2 %stage6.1 = (bf16[768,768]{1,0:T(8,128)(2,1)}, bf16[768,768]{1,0:T(8,128)(2,1)}, f32[3,256,256]{2,1,0:T(8,128)}) custom-call(f32[768,768]{1,0:T(8,128)} %get-tuple-element.36.refs_0_), custom_call_target="tpu_custom_call" | custom-call | flops 40000000000 | bytes 4718592 | tf_op jit(solution)/shard_map/stage6/pallas_call | solution.py:651
  297.4 9.6 %all-reduce.2.cloned.1.call-done.refs_10_ = f32[2304,128]{1,0:T(8,128)} async-done(((f32[2304,128]{1,0:T(8,128)}), f32[2304,128]{1,0:T(8,128)}) %all-reduce.2.cloned.1.call-update) | async-done | bytes 1179664 | tf_op jit(solution)/shard_map/psum | solution.py:753
  307.0 20.9 %solve.1 = (f32[32,2304]{1,0:T(8,128)}, f32[2304,128]{1,0:T(8,128)}) custom-call(bf16[768,2304]{1,0:T(8,128)(2,1)} %get-tuple-element.24.refs_0_, bf16[768,2304]{1,0:T(8,128)(2,1)} %get-tuple-element.25.refs_1_, f32[3,256,256]{2,1,0:T(8,128)} %get-tuple-element.26.refs_2_, bf16[768,1536]{1,0:T(8,128)(2,1)} %get-tuple-element.31.refs_3_, ...), custom_call_target="tpu_custom_call" | custom-call | tf_op jit(solution)/shard_map/solve/pallas_call | solution.py:708
  327.9 1.7 constant_dynamic-slice_fusion
Async XLA Ops:
  8.0 201.3 %all-gather.3.cloned.1.call-start = ((), (), s32[]{:S(2)}) async-start(), calls=%async_computation.3 | async-start | bytes 6340608 | tf_op jit(solution)/shard_map/all_gather | solution.py:746
  137.1 125.1 %reduce-scatter.2.cloned.1.call-start = ((), (), s32[]{:S(2)}) async-start(), calls=%async_computation.1 | async-start | bytes 5898240 | tf_op jit(solution)/shard_map/reduce_scatter | solution.py:750
  209.1 97.9 %all-reduce.2.cloned.1.call-start = ((), (), s32[]{:S(2)}) async-start(), calls=%async_computation.2 | async-start | bytes 2359296 | tf_op jit(solution)/shard_map/psum | solution.py:753
Sparse Core Ops, SparseCore 0:
  137.2 66.0 all-gather.2
Sparse Core Ops, SparseCore 1:
  209.2 48.8 reduce-scatter.1
  262.3 44.7 all-reduce.1

commit v6 on v5

--- a/solution.py
+++ b/solution.py
@@ -13,6 +13,7 @@
 F32, BF16 = jnp.float32, jnp.bfloat16
 TILE = 256
 HALF = 128
+TASKS = 7
 VMEM_LIMIT = 60 << 20
 WHOLE = pl.BlockSpec(memory_space=pltpu.VMEM)
 
@@ -447,7 +448,7 @@
     )(gate, left, right, omega)
 
 
-def leaf(rows):
+def leaf(rows, task=None, tasks=0):
     lane = lax.broadcasted_iota(jnp.int32, (8, HALF), 1)
     sub = lax.broadcasted_iota(jnp.int32, (8, HALF), 0)
     rows = list(rows)
@@ -472,6 +473,8 @@
                 mrow = jnp.broadcast_to(cols[m][k : k + 1, :], (8, HALF))
                 cols[m] = jnp.where(at, mrow * inv, cols[m] - factor * mrow)
         done.append(jnp.where(lane < base + 8, tri, 0.0))
+        for extra in range(j * tasks // count, (j + 1) * tasks // count):
+            task(extra)
         if j + 1 < count:
             prow = [jnp.broadcast_to(part[k : k + 1, :], (8, HALF)) for k in range(8)]
             for i in range(j + 1, count):
@@ -495,8 +498,8 @@
     refs = refs[3:]
     last = stop == nt
     out_ref = None if last else refs.pop(0)
-    grid_ref, a_ref, l_ref, uab_ref, sem = refs[:5]
-    extra_ref = refs[5] if has_carry and has_tiles else None
+    grid_ref, a_ref, l_ref, uab_ref, s3_ref, t3_ref, sem = refs[:7]
+    extra_ref = refs[7] if has_carry and has_tiles else None
     m = (nt - first) * TILE
     size = nt - first
     count = stop - first
@@ -541,6 +544,31 @@
 
         lax.fori_loop(0, size, add_row, 0)
 
+    def in_row(r):
+        return (size - r + 1) // 2
+
+    def total_tasks(p):
+        left = size - 1 - p
+        pairs = left // 2
+        count = jnp.where(left % 2 == 0, pairs * (pairs + 1), (pairs + 1) * (pairs + 1)) - 1
+        return jnp.where((p < 0) | (left < 1), 0, count)
+
+    def apply(r, q):
+        rat = pl.multiple_of(r * TILE, TILE)
+        cat = pl.multiple_of((size - 2 - 2 * q) * TILE, TILE)
+        t_ref[pl.ds(rat, TILE), pl.ds(cat, 2 * TILE)] -= jnp.dot(
+            t3_ref[pl.ds(rat, TILE), :], s3_ref[:, pl.ds(cat, 2 * TILE)], preferred_element_type=F32
+        )
+
+    def update(p, at):
+        row, begin, start = p + 1, jnp.int32(0), in_row(p + 1) - 1
+        for _ in range(size - 2):
+            nxt = at >= start
+            begin = jnp.where(nxt, start, begin)
+            row = jnp.where(nxt, row + 1, row)
+            start = jnp.where(nxt, start + in_row(row), start)
+        apply(row, at - begin)
+
     def half(p, h, carry):
         base = pl.multiple_of(p * TILE, TILE)
         mid = pl.multiple_of(p * TILE + HALF, HALF)
@@ -553,9 +581,26 @@
         def _():
             a_ref[...] = t_ref[pl.ds(mid, HALF), pl.ds(mid, HALF)] - tdot(uab_ref[...], uab_ref[...], HI)
 
-        out = leaf([a_ref[8 * i : 8 * i + 8, :] for i in range(HALF // 8)])
-        for i, rows in enumerate(out):
-            l_ref[8 * i : 8 * i + 8, :] = rows
+        done = carry
+        busy = done + TASKS <= total_tasks(p - 1) if size > 4 else False
+
+        def factor(task=None, tasks=0):
+            out = leaf([a_ref[8 * i : 8 * i + 8, :] for i in range(HALF // 8)], task, tasks)
+            for i, rows in enumerate(out):
+                l_ref[8 * i : 8 * i + 8, :] = rows
+
+        if size > 4:
+
+            @pl.when(busy)
+            def _():
+                factor(lambda extra: update(p - 1, done + extra), TASKS)
+
+            @pl.when(jnp.logical_not(busy))
+            def _():
+                factor()
+
+        else:
+            factor()
 
         @pl.when(h == 0)
         def _():
@@ -571,11 +616,17 @@
             inv_ref[p, HALF:, 0:HALF] = -jnp.dot(l_ref[...], cross, precision=HI)
             inv_ref[p, HALF:, HALF:] = l_ref[...]
 
-        return carry
+        return jnp.where(busy, done + TASKS, done)
 
     def panel(p, carry):
         base = pl.multiple_of(p * TILE, TILE)
-        lax.fori_loop(0, 2, functools.partial(half, p), 0)
+        done = lax.fori_loop(0, 2, functools.partial(half, p), jnp.int32(0))
+
+        def rest(at, carry):
+            update(p - 1, at)
+            return carry
+
+        lax.fori_loop(done, total_tasks(p - 1), rest, 0)
 
         def row_tile(c, carry):
             at = pl.multiple_of(c * TILE, TILE)
@@ -583,33 +634,28 @@
             head, rest = split(u)
             uh_ref[pl.ds(base, TILE), pl.ds(at, TILE)] = head
             ul_ref[pl.ds(base, TILE), pl.ds(at, TILE)] = rest
+            for third, value in enumerate((head, rest, head)):
+                s3_ref[third * TILE : (third + 1) * TILE, pl.ds(at, TILE)] = value
+            for third, value in enumerate((head.T, head.T, rest.T)):
+                t3_ref[pl.ds(at, TILE), third * TILE : (third + 1) * TILE] = value
             return carry
 
         lax.fori_loop(p + 1, size, row_tile, 0)
 
-        def trail_row(r, carry):
-            rat = pl.multiple_of(r * TILE, TILE)
-            head = uh_ref[pl.ds(base, TILE), pl.ds(rat, TILE)].T
-            rest = ul_ref[pl.ds(base, TILE), pl.ds(rat, TILE)].T
-
-            def trail(c, carry):
-                cat = pl.multiple_of(c * TILE, TILE)
-                ch = uh_ref[pl.ds(base, TILE), pl.ds(cat, TILE)]
-                cl = ul_ref[pl.ds(base, TILE), pl.ds(cat, TILE)]
-                update = jnp.dot(head, ch, preferred_element_type=F32) + (
-                    jnp.dot(head, cl, preferred_element_type=F32)
-                    + jnp.dot(rest, ch, preferred_element_type=F32)
-                )
-                t_ref[pl.ds(rat, TILE), pl.ds(cat, TILE)] -= update
-                return carry
-
-            lax.fori_loop(r, size, trail, 0)
+        @pl.when(p + 1 < size)
+        def _():
+            apply(p + 1, in_row(p + 1) - 1)
+
+        return carry
+
+    lax.fori_loop(0, count, panel, 0)
+    if not last:
+
+        def rest(at, carry):
+            update(count - 1, at)
             return carry
 
-        lax.fori_loop(p + 1, size, trail_row, 0)
-        return carry
-
-    lax.fori_loop(0, count, panel, 0)
+        lax.fori_loop(0, total_tasks(count - 1), rest, 0)
     if out_ref is not None:
         back = []
         for i in range(count, size):
@@ -643,6 +689,8 @@
         pltpu.VMEM((HALF, HALF), F32),
         pltpu.VMEM((HALF, HALF), F32),
         pltpu.VMEM((HALF, HALF), F32),
+        pltpu.VMEM((3 * TILE, m), BF16),
+        pltpu.VMEM((m, 3 * TILE), BF16),
         pltpu.SemaphoreType.DMA((2,)),
     ]
     if len(args) == 2:
@@ -658,7 +706,6 @@
         cost_estimate=pl.CostEstimate(
             flops=40 * 10**9, bytes_accessed=rows * m * 8, transcendentals=0
         ),
-        name=f"stage{first}",
     )(*args)
 
 
@@ -744,10 +791,9 @@
     )
     early = early.reshape((ny * nx * nz * nc,) + early.shape[4:])
     late = lax.all_gather(late[None], ("row", "x", "z", "core"), axis=0, tiled=True)
+    weights = lax.psum_scatter(weights, "x", scatter_dimension=0, tiled=True)
 
     *part_a, carry = stage(*CUTS[0], n, per, chunks, tiles=early)
-    carry, weights = lax.optimization_barrier((carry, weights))
-    weights = lax.psum_scatter(weights, "x", scatter_dimension=0, tiled=True)
     *part_b, carry = stage(*CUTS[1], n, per, chunks, tiles=late, carry=carry)
     carry, weights = lax.optimization_barrier((carry, weights))
     weights = lax.psum(weights, "row").reshape(n, width)
@@ -766,4 +812,6 @@
     col = ("x", "z", "core")
     in_specs = (P("row", col), P("row", col), P(), P(None, "row"))
     out_specs = (P(("row",) + col, None), P("row", col))
-    return jax.shard_map(on_device, mesh=fine, in_specs=in_specs, out_specs=out_specs, check_vma=False)
+    return jax.shard_map(
+        on_device, mesh=fine, in_specs=in_specs, out_specs=out_specs, check_vma=False
+    )

time: 337 us -> 355 us (1.053)
  waiting for transfers between devices: 9.71 us -> 46.3 us
  Pallas kernels: 310 us -> 291 us
    all_gather x1, waiting for transfers between devices: 0.02 us -> 36.4 us  [on_device(): lax.all_gather(late[None], ('row', 'x', 'z', 'core'), axis=0, tiled=True)]
    pallas_call x3, Pallas kernels: 160 us -> 141 us  [stage(): pl.pallas_call(functools.partial(stage_kernel, plan, per), out_shape=tupl...]
  transfers between devices with their start and end apart: 3 -> 3, of which waited for: 1 -> 2; matrix products, arithmetic and copies ran while one was open for 0% -> 0% of each run, Pallas kernels for 47% -> 40%
where the time goes in v6:
time: 355 us
  Pallas kernels  291 us (82%)
  waiting for transfers between devices  46.3 us (13%)
  between operations  15.5 us (4%)
    pallas_call x3, Pallas kernels, stage(): pl.pallas_call(functools.partial(stage_kernel, plan, per), out_shape=tupl...  141 us
    pallas_call x1, Pallas kernels, front(): pl.pallas_call(functools.partial(front_kernel, sizes, per, scale, cross_s...  129 us
    all_gather x1, waiting for transfers between devices, on_device(): lax.all_gather(late[None], ('row', 'x', 'z', 'core'), axis=0, tiled=True)  36.4 us
    pallas_call x1, Pallas kernels, solve(): pl.pallas_call(functools.partial(solve_kernel, plan), out_shape=(jax.Shap...  20.9 us
    psum x1, waiting for transfers between devices, on_device(): weights = lax.psum(weights, 'row').reshape(n, width)  9.34 us
  transfers between devices with their start and end apart: 3, of which 2 were waited for; matrix products, arithmetic and copies ran while one was open for 0% of the time, Pallas kernels for 40%

profile of v6, /device:TPU:0, one launch (start us, length us, event | category | flops | bytes accessed | tf_op | source)
XLA Modules:
  0.0 354.6 jit_solution(7017266189271579431)
XLA Ops:
  8.0 0.0 all-gather.3.cloned.1.call-start
  8.0 129.0 %front.1 = (f32[32,2304]{1,0:T(8,128)}, f32[4,4,4,2,3,16,256]{6,5,4,3,2,1,0:T(8,128)}, f32[3,16,256]{2,1,0:T(8,128)}, f32[4,2304,128]{2,1,0:T(8,128)}) custom-call(f32[4,4]{1,0:T(4,128)} %gate_ref.1, bf16[64,1024]{1,0:T(8,128)(2,1)} %bitcast.7, bf16[512,128]{1,0:T(8,128)(2,1)} %right_ref.1, bf16[576,4096]{1,0:T(8,128)(2,1)} %bitcast.5), custom_call_target="tpu_custom_call" | custom-call | tf_op jit(solution)/shard_map/front/pallas_call | solution.py:421
  137.0 0.0 all-gather.3.cloned.1.call-update
  137.1 0.0 reduce-scatter.2.cloned.1.call-start
  137.1 0.5 reduce-scatter.2.cloned.1.call-update
  137.6 0.2 all-reduce.2.cloned.1.call-start
  137.9 56.9 %shard_map.59 = (bf16[768,2304]{1,0:T(8,128)(2,1)}, bf16[768,2304]{1,0:T(8,128)(2,1)}, f32[3,256,256]{2,1,0:T(8,128)}, f32[1536,1536]{1,0:T(8,128)}) custom-call(f32[128,3,16,256]{3,2,1,0:T(8,128)} %bitcast.9), custom_call_target="tpu_custom_call" | custom-call | flops 40000000000 | bytes 14155776 | tf_op jit(solution)/shard_map/pallas_call | solution.py:699
  194.8 36.4 %all-gather.3.cloned.1.call-done = f32[384,16,256]{2,1,0:T(8,128)} async-done(((f32[3,16,256]{2,1,0:T(8,128)}), f32[384,16,256]{2,1,0:T(8,128)}) %all-gather.3.cloned.1.call-update) | async-done | bytes 6291472 | tf_op jit(solution)/shard_map/all_gather | solution.py:793
  231.2 48.8 %shard_map.60 = (bf16[768,1536]{1,0:T(8,128)(2,1)}, bf16[768,1536]{1,0:T(8,128)(2,1)}, f32[3,256,256]{2,1,0:T(8,128)}, f32[768,768]{1,0:T(8,128)}) custom-call(f32[128,3,16,256]{3,2,1,0:T(8,128)} %bitcast.8, f32[1536,1536]{1,0:T(8,128)} %get-tuple-element.26.refs_1_), custom_call_target="tpu_custom_call" | custom-call | flops 40000000000 | bytes 9437184 | tf_op jit(solution)/shard_map/pallas_call | solution.py:699
  280.0 0.0 reduce-scatter.2.cloned.1.call-done
  280.0 0.0 all-reduce.2.cloned.1.call-update
  280.0 35.2 %shard_map.61 = (bf16[768,768]{1,0:T(8,128)(2,1)}, bf16[768,768]{1,0:T(8,128)(2,1)}, f32[3,256,256]{2,1,0:T(8,128)}) custom-call(f32[768,768]{1,0:T(8,128)} %get-tuple-element.32.refs_0_), custom_call_target="tpu_custom_call" | custom-call | flops 40000000000 | bytes 4718592 | tf_op jit(solution)/shard_map/pallas_call | solution.py:699
  315.2 9.3 %all-reduce.2.cloned.1.call-done.refs_10_ = f32[2304,128]{1,0:T(8,128)} async-done(((f32[2304,128]{1,0:T(8,128)}), f32[2304,128]{1,0:T(8,128)}) %all-reduce.2.cloned.1.call-update) | async-done | bytes 1179664 | tf_op jit(solution)/shard_map/psum | solution.py:799
  324.6 20.9 %solve.1 = (f32[32,2304]{1,0:T(8,128)}, f32[2304,128]{1,0:T(8,128)}) custom-call(bf16[768,2304]{1,0:T(8,128)(2,1)} %get-tuple-element.22.refs_0_, bf16[768,2304]{1,0:T(8,128)(2,1)} %get-tuple-element.23.refs_1_, f32[3,256,256]{2,1,0:T(8,128)} %get-tuple-element.24.refs_2_, bf16[768,1536]{1,0:T(8,128)(2,1)} %get-tuple-element.27.refs_3_, ...), custom_call_target="tpu_custom_call" | custom-call | tf_op jit(solution)/shard_map/solve/pallas_call | solution.py:755
  345.4 1.7 constant_dynamic-slice_fusion
Async XLA Ops:
  8.0 223.2 %all-gather.3.cloned.1.call-start = ((), (), s32[]{:S(2)}) async-start(), calls=%async_computation.3 | async-start | bytes 6340608 | tf_op jit(solution)/shard_map/all_gather | solution.py:793
  137.1 142.9 %reduce-scatter.2.cloned.1.call-start = ((), (), s32[]{:S(2)}) async-start(), calls=%async_computation.1 | async-start | bytes 5898240 | tf_op jit(solution)/shard_map/reduce_scatter | solution.py:794
  137.6 186.9 %all-reduce.2.cloned.1.call-start = ((), (), s32[]{:S(2)}) async-start(), calls=%async_computation.2 | async-start | bytes 2359296 | tf_op jit(solution)/shard_map/psum | solution.py:799
Sparse Core Ops, SparseCore 0:
  137.2 93.9 all-gather.2
Sparse Core Ops, SparseCore 1:
  139.9 49.3 reduce-scatter.1
  280.1 44.4 all-reduce.1

commit v7 on v6

--- a/solution.py
+++ b/solution.py
@@ -734,7 +734,6 @@
             local = slice((p - first) * TILE, (p - first + 1) * TILE)
             y = jnp.dot(inv_ref[p - first], y_ref[rows, :], precision=HI)
             y_ref[rows, :] = y
-            proj_ref[rows, :] = y[:, HALF:]
             head, rest = split(y)
 
             def tail(r, carry):
@@ -747,6 +746,9 @@
 
             lax.fori_loop(p + 1, nt, tail, 0)
     basis_ref[...] = y_ref[:, :HALF].T[:mine]
+    block = proj_ref.shape[0]
+    at = pl.multiple_of(lax.axis_index("row") * block, block)
+    proj_ref[...] = y_ref[pl.ds(at, block), HALF:]
 
 
 def solve(plan, factors, sketch, weights):
@@ -754,7 +756,7 @@
     flat = [v for part in factors for v in part]
     return pl.pallas_call(
         functools.partial(solve_kernel, plan),
-        out_shape=(jax.ShapeDtypeStruct((mine, n), F32), jax.ShapeDtypeStruct((n, HALF), F32)),
+        out_shape=(jax.ShapeDtypeStruct((mine, n), F32), jax.ShapeDtypeStruct((n // lax.axis_size("row"), HALF), F32)),
         in_specs=[pl.BlockSpec(memory_space=pl.ANY)] * len(flat) + [WHOLE, WHOLE],
         out_specs=(WHOLE, WHOLE),
         scratch_shapes=[pltpu.VMEM((n, 2 * HALF), F32)]
@@ -799,8 +801,7 @@
     weights = lax.psum(weights, "row").reshape(n, width)
     part_c = stage(*CUTS[2], n, per, chunks, carry=carry)
     basis, projected = solve(CUTS, (part_a, part_b, part_c), sketch, weights)
-    block = n // ny
-    return basis, lax.dynamic_slice_in_dim(projected, lax.axis_index("row") * block, block, 0)
+    return basis, projected
 
 
 def math_sqrt(value):

time: 355 us -> 352 us (level)
  no operation moved by 1% of the time
where the time goes in v7:
time: 352 us
  Pallas kernels  291 us (83%)
  waiting for transfers between devices  45.7 us (13%)
  between operations  15.5 us (4%)
    pallas_call x3, Pallas kernels, stage(): pl.pallas_call(functools.partial(stage_kernel, plan, per), out_shape=tupl...  141 us
    pallas_call x1, Pallas kernels, front(): pl.pallas_call(functools.partial(front_kernel, sizes, per, scale, cross_s...  129 us
    all_gather x1, waiting for transfers between devices, on_device(): lax.all_gather(late[None], ('row', 'x', 'z', 'core'), axis=0, tiled=True)  35.7 us
    pallas_call x1, Pallas kernels, solve(): pl.pallas_call(functools.partial(solve_kernel, plan), out_shape=(jax.Shap...  20.7 us
    psum x1, waiting for transfers between devices, on_device(): weights = lax.psum(weights, 'row').reshape(n, width)  9.41 us
  transfers between devices with their start and end apart: 3, of which 2 were waited for; matrix products, arithmetic and copies ran while one was open for 0% of the time, Pallas kernels for 40%

profile of v7, /device:TPU:0, one launch (start us, length us, event | category | flops | bytes accessed | tf_op | source)
XLA Modules:
  0.0 352.1 jit_solution(11719314677121777134)
XLA Ops:
  8.0 0.0 all-gather.3.cloned.1.call-start
  8.0 129.0 %front.1 = (f32[32,2304]{1,0:T(8,128)}, f32[4,4,4,2,3,16,256]{6,5,4,3,2,1,0:T(8,128)}, f32[3,16,256]{2,1,0:T(8,128)}, f32[4,2304,128]{2,1,0:T(8,128)}) custom-call(f32[4,4]{1,0:T(4,128)} %gate_ref.1, bf16[64,1024]{1,0:T(8,128)(2,1)} %bitcast.7, bf16[512,128]{1,0:T(8,128)(2,1)} %right_ref.1, bf16[576,4096]{1,0:T(8,128)(2,1)} %bitcast.5), custom_call_target="tpu_custom_call" | custom-call | tf_op jit(solution)/shard_map/front/pallas_call | solution.py:421
  137.0 0.0 all-gather.3.cloned.1.call-update
  137.0 0.0 reduce-scatter.2.cloned.1.call-start
  137.1 0.5 reduce-scatter.2.cloned.1.call-update
  137.6 0.2 all-reduce.2.cloned.1.call-start
  137.9 56.9 %shard_map.59 = (bf16[768,2304]{1,0:T(8,128)(2,1)}, bf16[768,2304]{1,0:T(8,128)(2,1)}, f32[3,256,256]{2,1,0:T(8,128)}, f32[1536,1536]{1,0:T(8,128)}) custom-call(f32[128,3,16,256]{3,2,1,0:T(8,128)} %bitcast.9), custom_call_target="tpu_custom_call" | custom-call | flops 40000000000 | bytes 14155776 | tf_op jit(solution)/shard_map/pallas_call | solution.py:699
  194.8 35.7 %all-gather.3.cloned.1.call-done = f32[384,16,256]{2,1,0:T(8,128)} async-done(((f32[3,16,256]{2,1,0:T(8,128)}), f32[384,16,256]{2,1,0:T(8,128)}) %all-gather.3.cloned.1.call-update) | async-done | bytes 6291472 | tf_op jit(solution)/shard_map/all_gather | solution.py:795
  230.5 48.9 %shard_map.60 = (bf16[768,1536]{1,0:T(8,128)(2,1)}, bf16[768,1536]{1,0:T(8,128)(2,1)}, f32[3,256,256]{2,1,0:T(8,128)}, f32[768,768]{1,0:T(8,128)}) custom-call(f32[128,3,16,256]{3,2,1,0:T(8,128)} %bitcast.8, f32[1536,1536]{1,0:T(8,128)} %get-tuple-element.24.refs_1_), custom_call_target="tpu_custom_call" | custom-call | flops 40000000000 | bytes 9437184 | tf_op jit(solution)/shard_map/pallas_call | solution.py:699
  279.4 0.0 reduce-scatter.2.cloned.1.call-done
  279.4 0.0 all-reduce.2.cloned.1.call-update
  279.4 35.1 %shard_map.61 = (bf16[768,768]{1,0:T(8,128)(2,1)}, bf16[768,768]{1,0:T(8,128)(2,1)}, f32[3,256,256]{2,1,0:T(8,128)}) custom-call(f32[768,768]{1,0:T(8,128)} %get-tuple-element.30.refs_0_), custom_call_target="tpu_custom_call" | custom-call | flops 40000000000 | bytes 4718592 | tf_op jit(solution)/shard_map/pallas_call | solution.py:699
  314.5 9.4 %all-reduce.2.cloned.1.call-done.refs_10_ = f32[2304,128]{1,0:T(8,128)} async-done(((f32[2304,128]{1,0:T(8,128)}), f32[2304,128]{1,0:T(8,128)}) %all-reduce.2.cloned.1.call-update) | async-done | bytes 1179664 | tf_op jit(solution)/shard_map/psum | solution.py:801
  324.0 20.7 %solve.1 = (f32[32,2304]{1,0:T(8,128)}, f32[576,128]{1,0:T(8,128)}) custom-call(bf16[768,2304]{1,0:T(8,128)(2,1)} %get-tuple-element.20.refs_0_, bf16[768,2304]{1,0:T(8,128)(2,1)} %get-tuple-element.21.refs_1_, f32[3,256,256]{2,1,0:T(8,128)} %get-tuple-element.22.refs_2_, bf16[768,1536]{1,0:T(8,128)(2,1)} %get-tuple-element.25.refs_3_, ...), custom_call_target="tpu_custom_call" | custom-call | tf_op jit(solution)/shard_map/solve/pallas_call | solution.py:757
Async XLA Ops:
  8.0 222.5 %all-gather.3.cloned.1.call-start = ((), (), s32[]{:S(2)}) async-start(), calls=%async_computation.3 | async-start | bytes 6340608 | tf_op jit(solution)/shard_map/all_gather | solution.py:795
  137.0 142.4 %reduce-scatter.2.cloned.1.call-start = ((), (), s32[]{:S(2)}) async-start(), calls=%async_computation.1 | async-start | bytes 5898240 | tf_op jit(solution)/shard_map/reduce_scatter | solution.py:796
  137.6 186.3 %all-reduce.2.cloned.1.call-start = ((), (), s32[]{:S(2)}) async-start(), calls=%async_computation.2 | async-start | bytes 2359296 | tf_op jit(solution)/shard_map/psum | solution.py:801
Sparse Core Ops, SparseCore 0:
  137.2 93.2 all-gather.2
Sparse Core Ops, SparseCore 1:
  139.9 49.3 reduce-scatter.1
  279.5 44.4 all-reduce.1
